TPU v7x, 32 devices: a whole 2x2x4 slice. The times are simulated.
32 devices in a mesh: dp: 8 (over z, y), mp: 4 (over x, core).
Axes of the slice: x: 2, y: 2, z: 4, core: 2. Of those that a mesh axis runs over, the one named last changes fastest.
Arguments:
- tokens: bfloat16 [16384, 768], P(('dp', 'mp')), may hold values from -6 to 6
- cotangent: bfloat16 [16384, 768], P(('dp', 'mp')), may hold values from -6 to 6
- norm1_gain: float32 [768], replicated, may hold values from 0.5 to 1.5
- w_query: bfloat16 [768, 768], P(None, 'mp'), may hold values from -0.21875 to 0.21875
- w_key: bfloat16 [768, 768], P(None, 'mp'), may hold values from -0.21875 to 0.21875
- w_value: bfloat16 [768, 768], P(None, 'mp'), may hold values from -0.21875 to 0.21875
- w_attn_out: bfloat16 [768, 768], P('mp'), may hold values from -1.796875 to 1.796875
- bias_table: float32 [32, 12], P(None, 'mp'), may hold values from -6 to 6
- norm2_gain: float32 [768], replicated, may hold values from 0.5 to 1.5
- w_router: bfloat16 [768, 64], replicated, may hold values from -0.109375 to 0.109375
- w_expert_in: bfloat16 [64, 768, 3072], P('dp', None, 'mp'), may hold values from -0.21875 to 0.21875
- w_expert_out: bfloat16 [64, 3072, 768], P('dp', 'mp'), may hold values from -18 to 18
- routes: int32 [16384, 1], P(('dp', 'mp')), may hold values from 0 to 63; in each aligned block of 512 rows (0 to 511, 512 to 1023, ...) at most 16 rows name the same one
- segments: int32 [8, 2048], P('dp'), may hold values from 0 to 7, never falling along the last dimension, each value on 1 to 1024 neighbouring positions
- buckets: int32 [4095], replicated, may hold values from 0 to 31
Outputs:
- mixed: bfloat16 [16384, 768], P(('dp', 'mp'))
- grad_tokens: bfloat16 [16384, 768], P(('dp', 'mp'))
- grad_norm1_gain: float32 [768], replicated
- grad_w_query: float32 [768, 768], P(None, 'mp')
- grad_w_key: float32 [768, 768], P(None, 'mp')
- grad_w_value: float32 [768, 768], P(None, 'mp')
- grad_w_attn_out: float32 [768, 768], P('mp')
- grad_bias_table: float32 [32, 12], P(None, 'mp')
- grad_norm2_gain: float32 [768], replicated
- grad_w_router: float32 [768, 64], replicated
- grad_w_expert_in: float32 [64, 768, 3072], P('dp', None, 'mp')
- grad_w_expert_out: float32 [64, 3072, 768], P('dp', 'mp')
Inputs may be any that keep to these rules, and one draw needn't show every extreme that they name: `routes`: among the 512 rows of one device at most 16 name the same expert, and in every draw some expert is named by exactly 16 rows of some device. `segments`: within a sequence the document numbers never fall; each document has 1 to 1024 positions, one exactly that many.
All inputs are finite; a program needn't handle non-finite values.
Results may differ from a plain program's by a relative error of at most 0.018.
Values may be sent and summed in bfloat16 or wider, within the bound.
No kernel may reach another device: no remote copies, remote signals or barrier semaphores. Data moves between devices by JAX's collectives and lax.ppermute only.
A program may use at most 256 MiB of HBM per device.

v0:
```python
import jax
import jax.numpy as jnp
from jax import lax
from jax.experimental import pallas as pl
from jax.experimental.pallas import tpu as pltpu
from jax.sharding import PartitionSpec as P

EPSILON = 1e-06
SCORE_SCALE = 0.125
MASKED = -1e30
LOWEST = -3e38
PRECISE = lax.Precision.HIGHEST
BLOCK = 256
LANES = 128
LONGEST = 1024
DIRECT = 8
GELU_A = 0.7978845608028654
GELU_B = 0.044715
VMEM_BYTES = 50 * 1024 * 1024
BF16 = jnp.bfloat16
F32 = jnp.float32


def params():
    return pltpu.CompilerParams(vmem_limit_bytes=VMEM_BYTES)


def cost(flops, nbytes):
    return pl.CostEstimate(flops=int(flops), bytes_accessed=int(nbytes), transcendentals=0)


def dot_nn(left, right):
    return lax.dot_general(left, right, (((1,), (0,)), ((), ())), preferred_element_type=F32)


def dot_nt(left, right):
    return lax.dot_general(left, right, (((1,), (1,)), ((), ())), preferred_element_type=F32)


def dot_tn(left, right):
    return lax.dot_general(left, right, (((0,), (0,)), ((), ())), preferred_element_type=F32)


def rms_scale(values):
    return lax.rsqrt(jnp.mean(values * values, axis=-1, keepdims=True) + EPSILON)


def norm_back(values, scale, gain, upstream):
    weighted = gain * upstream
    gain_grad = jnp.sum(upstream * values * scale, axis=0)
    input_grad = scale * weighted - values * scale * scale * scale * jnp.mean(
        weighted * values, axis=-1, keepdims=True
    )
    return (input_grad, gain_grad)


def bias_kernel(rows_ref, out_ref):
    diag = pl.program_id(1)
    start = pl.multiple_of(diag * BLOCK, BLOCK)
    window = rows_ref[0, :, pl.ds(start, 2 * BLOCK)]
    spread = jnp.broadcast_to(window, (BLOCK, 2 * BLOCK))
    rolled = pltpu.roll(spread, BLOCK + 1, 1, stride=1, stride_axis=0)
    out_ref[0, 0] = rolled[:, :BLOCK]


def bias_tiles(rows, diags):
    heads, _, width = rows.shape
    return pl.pallas_call(
        bias_kernel,
        out_shape=jax.ShapeDtypeStruct((heads, diags, BLOCK, BLOCK), F32),
        grid=(heads, diags),
        in_specs=[pl.BlockSpec((1, 1, width), lambda h, d: (h, 0, 0))],
        out_specs=pl.BlockSpec((1, 1, BLOCK, BLOCK), lambda h, d: (h, d, 0, 0)),
        compiler_params=params(),
        cost_estimate=cost(1e8, heads * diags * BLOCK * BLOCK * 4),
        name="bias_tiles",
    )(rows)


def head_masks(heads, head_dim, width):
    lane = lax.broadcasted_iota(jnp.int32, (BLOCK, width), 1)
    return [(lane >= h * head_dim) & (lane < (h + 1) * head_dim) for h in range(heads)]


def masked_heads(rows, masks):
    wide = rows.astype(F32)
    return [jnp.where(m, wide, 0.0).astype(BF16) for m in masks]


def attend_kernel(
    heads, head_dim, reach, lo_ref, hi_ref, pos_ref, q_ref, k_ref, vt_ref, bias_ref, segc_ref, segr_ref,
    out_ref, norm_ref, acc, top, total,
):
    i = pl.program_id(0)
    queries = masked_heads(q_ref[...], head_masks(heads, head_dim, q_ref.shape[1]))
    acc[...] = jnp.zeros_like(acc)
    top[...] = jnp.full_like(top, LOWEST)
    total[...] = jnp.zeros_like(total)

    def step(j, carry):
        there = pl.ds(pl.multiple_of(j * BLOCK, BLOCK), BLOCK)
        rows = pl.ds(pl.multiple_of(pos_ref[j] * BLOCK, BLOCK), BLOCK)
        keys = k_ref[rows, :]
        same = segc_ref[there, :] == segr_ref[...]
        for h in range(heads):
            part = slice(h * head_dim, (h + 1) * head_dim)
            scores = dot_nt(keys, queries[h]) + bias_ref[h, i - j + reach]
            scores = jnp.where(same, scores, MASKED)
            old = top[h : h + 1, :]
            new = jnp.maximum(old, jnp.max(scores, axis=0, keepdims=True))
            shrink = jnp.exp(old - new)
            weights = jnp.exp(scores - new)
            top[h : h + 1, :] = new
            total[h : h + 1, :] = total[h : h + 1, :] * shrink + jnp.sum(
                weights, axis=0, keepdims=True
            )
            acc[part, :] = acc[part, :] * shrink + dot_nn(vt_ref[part, rows], weights.astype(BF16))
        return carry

    lax.fori_loop(lo_ref[i], hi_ref[i], step, 0)
    for h in range(heads):
        part = slice(h * head_dim, (h + 1) * head_dim)
        acc[part, :] = acc[part, :] / total[h : h + 1, :]
    out_ref[...] = acc[...].T.astype(BF16)
    norm_ref[...] = top[...] + jnp.log(jnp.maximum(total[...], 1e-37))


def attend(qkv, value_t, tiles, seg_col, seg_row, spans, heads, head_dim):
    seq_length = qkv.shape[0]
    width = value_t.shape[0]
    blocks = seq_length // BLOCK
    reach = tiles.shape[1] // 2
    whole = lambda shape: pl.BlockSpec(shape, lambda i, lo, hi, pos: (0,) * len(shape))
    return pl.pallas_call(
        lambda *refs: attend_kernel(heads, head_dim, reach, *refs),
        out_shape=(
            jax.ShapeDtypeStruct((seq_length, width), BF16),
            jax.ShapeDtypeStruct((8, seq_length), F32),
        ),
        grid_spec=pltpu.PrefetchScalarGridSpec(
            num_scalar_prefetch=3,
            grid=(blocks,),
            in_specs=[
                pl.BlockSpec((BLOCK, width), lambda i, lo, hi, pos: (pos[i], 0)),
                pl.BlockSpec((seq_length, width), lambda i, lo, hi, pos: (0, 1)),
                whole(value_t.shape),
                whole(tiles.shape),
                whole(seg_col.shape),
                pl.BlockSpec((1, BLOCK), lambda i, lo, hi, pos: (0, i)),
            ],
            out_specs=(
                pl.BlockSpec((BLOCK, width), lambda i, lo, hi, pos: (pos[i], 0)),
                pl.BlockSpec((8, BLOCK), lambda i, lo, hi, pos: (0, i)),
            ),
            scratch_shapes=[
                pltpu.VMEM((width, BLOCK), F32),
                pltpu.VMEM((8, BLOCK), F32),
                pltpu.VMEM((8, BLOCK), F32),
            ],
        ),
        compiler_params=params(),
        cost_estimate=cost(2e10, 1.2e7),
        name="attend",
    )(*spans, qkv, qkv, value_t, tiles, seg_col, seg_row)


def attend_back_kernel(
    heads, head_dim, reach, first, lo_ref, hi_ref, pos_ref, q_ref, go_ref, out_ref, norm_ref, k_ref, kt_ref, v_ref,
    bias_ref, segc_ref, segr_ref, gq_ref, gk_ref, gv_ref, offs_ref, gqt, gk, gv, gbias,
):
    i = pl.program_id(0)

    @pl.when(i == 0)
    def _():
        gk[...] = jnp.zeros_like(gk)
        gv[...] = jnp.zeros_like(gv)
        gbias[...] = jnp.zeros_like(gbias)

    masks = head_masks(heads, head_dim, q_ref.shape[1])
    queries = masked_heads(q_ref[...], masks)
    grads = masked_heads(go_ref[...], masks)
    product = go_ref[...].astype(F32) * out_ref[...].astype(F32)
    pick = lax.broadcasted_iota(jnp.int32, (8, q_ref.shape[1]), 0)
    lane = lax.broadcasted_iota(jnp.int32, (8, q_ref.shape[1]), 1)
    pick = ((lane >= pick * head_dim) & (lane < (pick + 1) * head_dim)).astype(F32)
    inner = lax.dot_general(
        pick, product, (((1,), (1,)), ((), ())), precision=PRECISE, preferred_element_type=F32
    )
    gqt[...] = jnp.zeros_like(gqt)

    def step(j, carry):
        there = pl.ds(pl.multiple_of(j * BLOCK, BLOCK), BLOCK)
        rows = pl.ds(pl.multiple_of(pos_ref[j] * BLOCK, BLOCK), BLOCK)
        keys = k_ref[rows, :]
        values = v_ref[rows, :]
        same = segc_ref[there, :] == segr_ref[...]
        for h in range(heads):
            part = slice(h * head_dim, (h + 1) * head_dim)
            scores = dot_nt(keys, queries[h]) + bias_ref[h, i - j + reach]
            weights = jnp.exp(jnp.where(same, scores, MASKED) - norm_ref[first + h : first + h + 1, :])
            slope = weights * (dot_nt(values, grads[h]) - inner[h : h + 1, :])
            gbias[h, i - j + reach] += slope
            low_slope = slope.astype(BF16)
            gv[rows, :] += dot_nn(weights.astype(BF16), grads[h])
            gk[rows, :] += dot_nn(low_slope, queries[h])
            gqt[part, :] += dot_nn(kt_ref[part, rows], low_slope)
        return carry

    lax.fori_loop(lo_ref[i], hi_ref[i], step, 0)
    gq_ref[...] = (gqt[...] * SCORE_SCALE).T.astype(BF16)

    @pl.when(i == pl.num_programs(0) - 1)
    def _():
        gk_ref[...] = gk[...].astype(BF16)
        gv_ref[...] = gv[...].astype(BF16)
        offs_ref[...] = jnp.zeros_like(offs_ref)
        blank = jnp.zeros((BLOCK, BLOCK), F32)
        for h in range(heads):
            for d in range(2 * reach + 1):
                sums = jnp.concatenate([gbias[h, d], blank], axis=1)
                size = BLOCK // 2
                while size >= 8:
                    sums = pltpu.roll(sums[:size], size, 1) + sums[size:]
                    size //= 2
                line = sums[7:8]
                for r in range(7):
                    line = line + pltpu.roll(sums[r : r + 1], 7 - r, 1)
                offs_ref[h : h + 1, d * BLOCK : (d + 2) * BLOCK] += line


def attend_back(
    group, heads, head_dim, qkv, grad_heads, head_out, norms, key_t, tiles, seg_col, seg_row, spans,
    ready,
):
    seq_length = qkv.shape[0]
    groups = head_out.shape[1] // LANES
    blocks = seq_length // BLOCK
    diags = tiles.shape[1]
    reach = diags // 2
    first = group * (LANES // head_dim)
    count = min(heads - first, LANES // head_dim)
    whole = lambda shape: pl.BlockSpec(shape, lambda i, lo, hi, pos: (0,) * len(shape))
    row_block = pl.BlockSpec((BLOCK, LANES), lambda i, lo, hi, pos: (pos[i], group))
    columns = lambda n: pl.BlockSpec((seq_length, LANES), lambda i, lo, hi, pos: (0, n * groups + group))
    rows_out = jax.ShapeDtypeStruct((seq_length, LANES), BF16)
    offsets = jax.ShapeDtypeStruct((8, (diags + 1) * BLOCK), F32)
    return pl.pallas_call(
        lambda *refs: attend_back_kernel(
            count, head_dim, reach, first, *refs[:13], *refs[13 + len(ready) :]
        ),
        out_shape=(rows_out, rows_out, rows_out, offsets),
        grid_spec=pltpu.PrefetchScalarGridSpec(
            num_scalar_prefetch=3,
            grid=(blocks,),
            in_specs=[
                row_block,
                row_block,
                row_block,
                pl.BlockSpec((8, BLOCK), lambda i, lo, hi, pos: (0, i)),
                columns(1),
                pl.BlockSpec((LANES, seq_length), lambda i, lo, hi, pos: (group, 0)),
                columns(2),
                pl.BlockSpec(
                    (count,) + tiles.shape[1:], lambda i, lo, hi, pos: (first // count, 0, 0, 0)
                ),
                whole(seg_col.shape),
                pl.BlockSpec((1, BLOCK), lambda i, lo, hi, pos: (0, i)),
            ]
            + [pl.BlockSpec(memory_space=pl.ANY)] * len(ready),
            out_specs=(
                pl.BlockSpec((BLOCK, LANES), lambda i, lo, hi, pos: (pos[i], 0)),
                whole(rows_out.shape),
                whole(rows_out.shape),
                whole(offsets.shape),
            ),
            scratch_shapes=[
                pltpu.VMEM((LANES, BLOCK), F32),
                pltpu.VMEM((seq_length, LANES), F32),
                pltpu.VMEM((seq_length, LANES), F32),
                pltpu.VMEM((count, diags, BLOCK, BLOCK), F32),
            ],
        ),
        compiler_params=params(),
        cost_estimate=cost(1.4e10 * count, 5e6 * count),
        name="attend_back",
    )(*spans, qkv, grad_heads, head_out, norms, qkv, key_t, qkv, tiles, seg_col, seg_row, *ready)


def split_rows(refs):
    parts = [r[...].reshape(-1, r.shape[-1]) for r in refs]
    return jnp.concatenate(parts, axis=0)


def store_rows(refs, values):
    size = values.shape[0] // len(refs)
    for n, r in enumerate(refs):
        r[...] = values[n * size : (n + 1) * size].astype(r.dtype).reshape(r.shape)


def expert_kernel(groups, *refs):
    xs, us = refs[:groups], refs[groups : 2 * groups]
    win_ref, wout_ref, wr_ref, hot_ref = refs[2 * groups : 2 * groups + 4]
    outs = refs[2 * groups + 4 : 3 * groups + 4]
    act_ref, gpre_ref, gu_ref, gl_ref = refs[3 * groups + 4 :]
    hot = hot_ref[0]
    size = act_ref.shape[2] // 2
    for n in range(2):
        part = slice(n * groups // 2, (n + 1) * groups // 2)
        rows = slice(n * size, (n + 1) * size)
        x = split_rows(xs[part])
        u = split_rows(us[part])
        logits = dot_nn(x, wr_ref[...])
        powers = jnp.exp(logits - jnp.max(logits, axis=-1, keepdims=True))
        probs = powers / jnp.sum(powers, axis=-1, keepdims=True)
        gate = jnp.sum(probs * hot, axis=-1, keepdims=True)
        pre = dot_nn(x, win_ref[0])
        back = dot_nt(u, wout_ref[0])
        square = pre * pre
        bent = jnp.tanh(pre * (GELU_A + GELU_A * GELU_B * square))
        half = 0.5 + 0.5 * bent
        act = (pre * half).astype(BF16)
        slope = half + pre * (0.5 - 0.5 * bent * bent) * (GELU_A + 3.0 * GELU_A * GELU_B * square)
        grad_gate = jnp.sum(act.astype(F32) * back, axis=-1, keepdims=True)
        grad_pre = (gate * back * slope).astype(BF16)
        grad_logits = grad_gate * gate * (hot - probs)
        high = grad_logits.astype(BF16)
        rest = (grad_logits - high.astype(F32)).astype(BF16)
        grad_x = dot_nt(grad_pre, win_ref[0]) + dot_nt(high, wr_ref[...])
        store_rows(outs[part], grad_x + dot_nt(rest, wr_ref[...]))
        act_ref[0, 0, rows] = act
        gpre_ref[0, 0, rows] = grad_pre
        gu_ref[0, 0, rows] = (gate * u.astype(F32)).astype(BF16)
        gl_ref[0, 0, rows] = grad_logits


def slot_specs(groups, tile, capacity, width, first=0):
    spec = pl.BlockSpec((tile, 1, capacity, width), lambda e, t: (t, e + first, 0, 0))
    return [spec] * groups


def experts(xs, us, w_in, w_out, w_router, hots, first):
    groups = len(xs)
    sources, count, capacity, width = xs[0].shape
    tile = min(sources, DIRECT)
    tiles = sources // tile
    rows = groups * tile * capacity
    hidden_units = w_in.shape[2]
    slots = slot_specs(groups, tile, capacity, width)
    kept = lambda last: pl.BlockSpec((1, 1, rows, last), lambda e, t: (e, t, 0, 0))
    kept_shape = lambda last, dt: jax.ShapeDtypeStruct((count, tiles, rows, last), dt)
    expert_count = w_router.shape[1]
    res = pl.pallas_call(
        lambda *refs: expert_kernel(groups, *refs),
        out_shape=[jax.ShapeDtypeStruct(xs[0].shape, BF16)] * groups
        + [
            kept_shape(hidden_units, BF16),
            kept_shape(hidden_units, BF16),
            kept_shape(width, BF16),
            kept_shape(expert_count, F32),
        ],
        grid=(count, tiles),
        in_specs=slots
        + slot_specs(groups, tile, capacity, width, first)
        + [
            pl.BlockSpec((1, width, hidden_units), lambda e, t: (e + first, 0, 0)),
            pl.BlockSpec((1, hidden_units, width), lambda e, t: (e + first, 0, 0)),
            pl.BlockSpec(w_router.shape, lambda e, t: (0, 0)),
            pl.BlockSpec((1, 1, expert_count), lambda e, t: (e + first, 0, 0)),
        ],
        out_specs=slots + [kept(hidden_units), kept(hidden_units), kept(width), kept(expert_count)],
        compiler_params=params(),
        cost_estimate=cost(6 * count * tiles * rows * width * hidden_units, 7e6 * count),
        name="experts",
    )(*xs, *us, w_in, w_out, w_router, hots)
    return res[:groups], res[groups:]


def weight_kernel(groups, *refs):
    xs = refs[:groups]
    act_ref, gpre_ref, gu_ref, gl_ref, wout_ref = refs[groups : groups + 5]
    outs = refs[-groups - 3 : -3]
    gin_ref, gout_ref, gr_ref = refs[-3:]
    x = split_rows(xs)
    act = act_ref[0, 0]
    store_rows(outs, dot_nn(act, wout_ref[0]))
    grad_logits = gl_ref[0, 0]
    high = grad_logits.astype(BF16)
    rest = (grad_logits - high.astype(F32)).astype(BF16)
    first = pl.program_id(1) == 0

    @pl.when(first)
    def _():
        gin_ref[0] = dot_tn(x, gpre_ref[0, 0])
        gout_ref[0] = dot_tn(act, gu_ref[0, 0])

    @pl.when(jnp.logical_not(first))
    def _():
        gin_ref[0] += dot_tn(x, gpre_ref[0, 0])
        gout_ref[0] += dot_tn(act, gu_ref[0, 0])

    router = dot_tn(x, high) + dot_tn(x, rest)
    start = first & (pl.program_id(0) == 0)

    @pl.when(start)
    def _():
        gr_ref[...] = router

    @pl.when(jnp.logical_not(start))
    def _():
        gr_ref[...] += router


def expert_weights(xs, kept, w_out, first, earlier):
    groups = len(xs)
    sources, count, capacity, width = xs[0].shape
    tile = min(sources, DIRECT)
    tiles = sources // tile
    rows = groups * tile * capacity
    hidden_units = w_out.shape[1]
    expert_count = kept[3].shape[-1]
    slots = slot_specs(groups, tile, capacity, width)
    held = lambda last: pl.BlockSpec((1, 1, rows, last), lambda e, t: (e, t, 0, 0))
    anywhere = [pl.BlockSpec(memory_space=pl.ANY)] * len(earlier)
    inputs = groups + 5
    res = pl.pallas_call(
        lambda *refs: weight_kernel(groups, *refs),
        out_shape=[jax.ShapeDtypeStruct((sources, w_out.shape[0], capacity, width), BF16)] * groups
        + [
            jax.ShapeDtypeStruct((w_out.shape[0], width, hidden_units), F32),
            jax.ShapeDtypeStruct((w_out.shape[0], hidden_units, width), F32),
            jax.ShapeDtypeStruct((width, expert_count), F32),
        ],
        grid=(count, tiles),
        in_specs=slots
        + [held(hidden_units), held(hidden_units), held(width), held(expert_count)]
        + [pl.BlockSpec((1, hidden_units, width), lambda e, t: (e + first, 0, 0))]
        + anywhere,
        out_specs=slot_specs(groups, tile, capacity, width, first)
        + [
            pl.BlockSpec((1, width, hidden_units), lambda e, t: (e + first, 0, 0)),
            pl.BlockSpec((1, hidden_units, width), lambda e, t: (e + first, 0, 0)),
            pl.BlockSpec((width, expert_count), lambda e, t: (0, 0)),
        ],
        input_output_aliases={inputs + n: n for n in range(len(earlier))},
        compiler_params=params(),
        cost_estimate=cost(6 * count * tiles * rows * width * hidden_units, 1e7 * count),
        name="expert_weights",
    )(*xs, *kept, w_out, *earlier)
    return res[: groups + 2], res[groups + 2]


def after(values, *earlier):
    return lax.optimization_barrier((values,) + earlier)[0]


def swap(values, axis, step):
    count = lax.axis_size(axis)
    return lax.ppermute(values, axis, [(n, n ^ step) for n in range(count)])


def gather_mp(values):
    across = swap(values, "mp", 2)
    return [values, swap(values, "mp", 1), across, swap(across, "mp", 1)]


def fold_mp(parts):
    near = parts[0].astype(F32) + swap(parts[1], "mp", 1).astype(F32)
    far = parts[2].astype(F32) + swap(parts[3], "mp", 1).astype(F32)
    return near + swap(far.astype(BF16), "mp", 2).astype(F32)


def trade_dp(values):
    return lax.all_to_all(values, "dp", split_axis=0, concat_axis=0, tiled=True)


def trade_dp_steps(values):
    count = lax.axis_size("dp")
    if count > DIRECT:
        return trade_dp(values)
    own = lax.axis_index("dp")
    held, step = values[None], count // 2
    while step > 0:
        low = (own // step) % 2 == 0
        sent, size = held.shape[0], held.shape[1] // 2
        first, second = held[:, :size], held[:, size:]
        leave = jnp.where(low, second, first)
        came = swap(leave, "dp", step)
        stay = jnp.where(low, first, second)
        held = jnp.stack([jnp.where(low, stay, came), jnp.where(low, came, stay)], axis=1)
        held = held.reshape((2 * sent, size) + values.shape[1:])
        step //= 2
    return held[:, 0]


def sum_steps(values, axis):
    step = 1
    while step < lax.axis_size(axis):
        values = values + swap(values, axis, step)
        step *= 2
    return values


def fold_dp(values):
    count = lax.axis_size("dp")
    parts = values.reshape((count, values.shape[0] // count) + values.shape[1:])
    return jnp.sum(trade_dp(parts).astype(F32), axis=0)


def share_dp(pieces):
    mine = jnp.concatenate(pieces, axis=1).astype(BF16)
    count = lax.axis_size("dp")
    whole = trade_dp(jnp.broadcast_to(mine[None], (count,) + mine.shape))
    whole = whole.reshape(-1, mine.shape[1]).astype(F32)
    ends = [0]
    for p in pieces:
        ends.append(ends[-1] + p.shape[1])
    return [whole[:, a:b] for a, b in zip(ends, ends[1:])]


def per_device(
    tokens,
    cotangent,
    norm1_gain,
    w_query,
    w_key,
    w_value,
    w_attn_out,
    bias_table,
    norm2_gain,
    w_router,
    w_expert_in,
    w_expert_out,
    routes,
    segments,
    buckets,
):
    tok_rows, model_width = tokens.shape
    groups = lax.axis_size("mp")
    sources = lax.axis_size("dp")
    own_mp, own_dp = lax.axis_index("mp"), lax.axis_index("dp")
    seq_length = tok_rows * groups
    blocks = seq_length // BLOCK
    bucket_count, heads_local = bias_table.shape
    head_width = w_query.shape[1]
    expert_count = w_router.shape[1]
    capacity = 2 * tok_rows // expert_count
    exp_local = w_expert_in.shape[0]
    chunks = 2 if exp_local % 2 == 0 else 1
    chunk_experts = exp_local // chunks
    reach = min(LONGEST // BLOCK, blocks - 1)
    head_dim = head_width // heads_local
    lane_groups = -(-head_width // LANES)

    inputs = tokens.astype(F32)
    scale_one = rms_scale(inputs)
    normed_one = (inputs * scale_one * norm1_gain).astype(BF16)
    half = tok_rows // 2
    pieces = zip(gather_mp(normed_one[:half]), gather_mp(normed_one[half:]))
    normed_all = jnp.concatenate([part for pair in pieces for part in pair], axis=0)

    expert_of = routes[:, 0]
    chosen = expert_of[:, None] == jnp.arange(expert_count, dtype=jnp.int32)[None, :]
    positions = jnp.arange(tok_rows, dtype=jnp.int32)
    earlier = (positions[None, :] < positions[:, None]).astype(BF16)
    before = jnp.dot(earlier, chosen.astype(BF16), preferred_element_type=F32)
    slot_rank = jnp.sum(before * chosen.astype(F32), axis=-1).astype(jnp.int32)
    slot_index = expert_of * capacity + slot_rank
    slot_count = expert_count * capacity
    picks = (slot_index[:, None] == jnp.arange(slot_count, dtype=jnp.int32)[None, :]).astype(BF16)

    def to_slots(rows):
        slots = dot_tn(picks, rows).astype(BF16)
        return slots.reshape(sources, exp_local, capacity, model_width)

    offsets = jnp.concatenate([buckets[::-1], jnp.full((1,), -1, jnp.int32)])
    first = seq_length - (reach + 1) * BLOCK
    offsets = offsets[first : first + (2 * reach + 2) * BLOCK]
    bucket_hot = (
        offsets[None, :] == jnp.arange(bucket_count, dtype=jnp.int32)[:, None]
    ).astype(F32)
    bias_rows = jnp.dot(bias_table.T, bucket_hot, precision=PRECISE)
    tiles = bias_tiles(bias_rows[:, None, :], 2 * reach + 1)

    seg_all = segments[0]
    ends = seg_all.reshape(blocks, BLOCK)
    low = jnp.sum(seg_all[None, :] < ends[:, :1], axis=1, dtype=jnp.int32) // BLOCK
    high = -(-jnp.sum(seg_all[None, :] <= ends[:, -1:], axis=1, dtype=jnp.int32) // BLOCK)
    block_ids = jnp.arange(blocks, dtype=jnp.int32)
    low = jnp.maximum(low, block_ids - reach)
    high = jnp.minimum(high, block_ids + reach + 1)
    per = tok_rows // BLOCK
    spans = (low, high, (block_ids // per ^ own_mp) * per + block_ids % per)
    seg_col, seg_row = seg_all[:, None], seg_all[None, :]

    up_slots = trade_dp(to_slots(after(cotangent, normed_one)))

    spare = ((0, 0), (0, lane_groups * LANES - head_width))
    padded = [jnp.pad(w, spare) for w in (w_query, w_key, w_value)]
    scaled = jnp.concatenate([padded[0] * jnp.asarray(SCORE_SCALE, BF16)] + padded[1:], axis=1)
    qkv = jnp.dot(normed_all, scaled, preferred_element_type=F32).astype(BF16)
    value_t = qkv[:, 2 * padded[0].shape[1] :].T
    grad_slots = gather_mp(after(up_slots, normed_all))
    w_out_parts = gather_mp(after(w_attn_out, normed_all))
    head_out, norms = attend(
        qkv, value_t, tiles, seg_col, seg_row, spans, heads_local, head_dim
    )

    def block_of(rows, n):
        return rows[n * tok_rows : (n + 1) * tok_rows]

    head_rows = head_out[:, :head_width]
    head_parts = [block_of(head_rows, 0)] + [
        swap(block_of(head_rows, n), "mp", n) for n in range(1, groups)
    ]
    attn = jnp.dot(
        jnp.concatenate(head_parts, axis=1),
        jnp.concatenate(w_out_parts, axis=0),
        preferred_element_type=F32,
    )
    hidden = inputs + attn
    scale_two = rms_scale(hidden)
    normed_two = (hidden * scale_two * norm2_gain).astype(BF16)
    slots = trade_dp(to_slots(normed_two))
    token_slots = [
        gather_mp(slots[:, c * chunk_experts : (c + 1) * chunk_experts]) for c in range(chunks)
    ]

    hots = (
        (own_dp * exp_local + jnp.arange(exp_local, dtype=jnp.int32))[:, None]
        == jnp.arange(expert_count, dtype=jnp.int32)[None, :]
    ).astype(F32)[:, None, :]
    folded, kept = [], []
    for c in range(chunks):
        parts, extra = experts(
            token_slots[c], grad_slots, w_expert_in, w_expert_out, w_router, hots,
            c * chunk_experts,
        )
        folded.append(fold_mp(parts).astype(BF16))
        kept.append(extra)
    back = [trade_dp(f) for f in folded]
    grad_w_router, made = 0.0, ()
    for c in range(chunks):
        made, grad_router = expert_weights(
            token_slots[c], kept[c], w_expert_out, c * chunk_experts, made
        )
        grad_w_router = grad_w_router + grad_router
    grad_w_expert_in, grad_w_expert_out = made[groups:]
    far_rows = (made[2].astype(F32) + swap(made[3], "mp", 1).astype(F32)).astype(BF16)
    near_rows = made[0].astype(F32) + swap(made[1], "mp", 1).astype(F32)
    back = jnp.concatenate(back, axis=1).reshape(-1, model_width)
    grad_normed_two = jnp.dot(picks, after(back, grad_w_router), preferred_element_type=F32)

    upstream = cotangent.astype(F32)
    grad_hidden, grad_norm2_gain = norm_back(hidden, scale_two, norm2_gain, grad_normed_two)
    grad_hidden = grad_hidden + upstream
    grad_attn = grad_hidden.astype(BF16)

    grad_heads = [dot_nt(grad_attn, w).astype(BF16) for w in w_out_parts]
    grad_heads = [g if n == 0 else swap(g, "mp", n) for n, g in enumerate(grad_heads)]
    grad_heads = jnp.pad(jnp.concatenate(grad_heads, axis=0), spare)
    key_t = qkv[:, padded[0].shape[1] : 2 * padded[0].shape[1]].T

    shared = jnp.concatenate([grad_w_router, grad_norm2_gain[:, None]], axis=1)
    shared = sum_steps(after(shared, grad_attn), "mp")
    grad_attn_all = jnp.concatenate(gather_mp(after(grad_attn, grad_heads)), axis=0)
    rest = [dot_tn(grad_attn_all, head_rows), shared]
    folded_rows = (near_rows + swap(far_rows, "mp", 2).astype(F32)).astype(BF16)
    order, piece_of, bias_sums, gain_sum, summed = [], [], [], 0.0, []
    ready = [far_rows]
    for g in range(lane_groups):
        grad_q, grad_k, grad_v, offset_grad = attend_back(
            g, heads_local, head_dim, qkv, grad_heads, head_out, norms, key_t, tiles, seg_col,
            seg_row, spans, ready,
        )
        lanes = min(LANES, head_width - g * LANES)
        own = jnp.concatenate([grad_q[:, :lanes], grad_k[:, :lanes], grad_v[:, :lanes]], axis=1)
        weights = jnp.concatenate([w[:, g * LANES : g * LANES + lanes] for w in padded], axis=1)
        order.append((own, weights))
        partial = dot_tn(normed_all, own)
        gain_sum = gain_sum + jnp.sum(partial * weights.astype(F32), axis=1)
        payload = jnp.concatenate([partial] + rest, axis=1).astype(BF16)
        piece_of.append((lanes, payload.shape[1]))
        rest, ready = [], [payload, folded_rows]
        summed.append(fold_dp(payload))
        bias_sums.append(offset_grad[: lanes // head_dim])
    summed = share_dp(summed)
    grads = [[], [], []]
    for (lanes, _), columns in zip(piece_of, summed):
        for n in range(3):
            grads[n].append(columns[:, n * lanes : (n + 1) * lanes])
    grads = [jnp.concatenate(g, axis=1) for g in grads]
    rest = summed[0][:, 3 * piece_of[0][0] :]
    grad_w_attn_out, shared = rest[:, :head_width].T, rest[:, head_width:]

    rows_back = trade_dp_steps(folded_rows)
    router_logits = jnp.dot(normed_two, w_router, preferred_element_type=F32)
    router_exp = jnp.exp(router_logits - jnp.max(router_logits, axis=-1, keepdims=True))
    router_probs = router_exp / jnp.sum(router_exp, axis=-1, keepdims=True)
    gate_prob = jnp.sum(router_probs * chosen.astype(F32), axis=-1, keepdims=True)
    expert_rows = jnp.dot(picks, rows_back.reshape(-1, model_width), preferred_element_type=F32)
    mixed = (hidden + gate_prob * expert_rows).astype(BF16)

    own = jnp.concatenate([p[0] for p in order], axis=1)
    weights = jnp.concatenate([p[1] for p in order], axis=1)
    total = dot_nt(own, weights).astype(BF16)
    grad_normed_one = fold_mp([block_of(total, n) for n in range(groups)])
    bias_sums = jnp.dot(jnp.concatenate(bias_sums, axis=0), bucket_hot.T, precision=PRECISE)
    small = jnp.concatenate([gain_sum / norm1_gain, bias_sums.reshape(-1)])
    small = jnp.pad(small, (0, -small.shape[0] % (8 * LANES))).reshape(8, -1)
    small = sum_steps(small, "dp")
    grad_norm1_gain = sum_steps(small, "mp").reshape(-1)[:model_width]
    bias_sums = small.reshape(-1)[model_width : model_width + heads_local * bucket_count]
    grad_bias_table = bias_sums.reshape(heads_local, -1).T
    weighted = norm1_gain * grad_normed_one
    grad_inputs = scale_one * weighted - inputs * scale_one * scale_one * scale_one * jnp.mean(
        weighted * inputs, axis=-1, keepdims=True
    )
    grad_tokens = (grad_inputs + grad_hidden).astype(BF16)
    return (
        mixed,
        grad_tokens,
        grad_norm1_gain,
        *grads,
        grad_w_attn_out,
        grad_bias_table,
        shared[:, expert_count],
        shared[:, :expert_count],
        grad_w_expert_in,
        grad_w_expert_out,
    )


def solution(mesh):
    return jax.shard_map(
        per_device,
        mesh=mesh,
        in_specs=(
            P(("dp", "mp"), None),
            P(("dp", "mp"), None),
            P(),
            P(None, "mp"),
            P(None, "mp"),
            P(None, "mp"),
            P("mp", None),
            P(None, "mp"),
            P(),
            P(),
            P("dp", None, "mp"),
            P("dp", "mp", None),
            P(("dp", "mp"), None),
            P("dp", None),
            P(),
        ),
        out_specs=(
            P(("dp", "mp"), None),
            P(("dp", "mp"), None),
            P(),
            P(None, "mp"),
            P(None, "mp"),
            P(None, "mp"),
            P("mp", None),
            P(None, "mp"),
            P(),
            P(),
            P("dp", None, "mp"),
            P("dp", "mp", None),
        ),
        check_vma=False,
    )
```

profile of v0, /device:TPU:0, one launch (start us, length us, event | category | flops | bytes accessed | tf_op | source)
XLA Modules:
  0.0 509.7 jit_solution(11286475567424659473)
XLA Ops:
  10.5 6.2 %all-to-all-start.1 = ((bf16[8,8,16,768]{3,2,1,0:T(8,128)(2,1)}), bf16[8,8,16,768]{3,2,1,0:T(8,128)(2,1)}, u32[]{:S(2)}, u32[]{:S(2)}) async-start(bf16[8,8,16,768]{3,2,1,0:T(8,128)(2,1)} %bitcast.10), calls=%async_computation.1 | async-start | bytes 3145728 | tf_op jit(solution)/shard_map/all_to_all | solution.py:473
  20.0 11.9 %bias_tiles.1.refs_6_.refs_10_ = f32[3,9,256,256]{3,2,1,0:T(8,128)} custom-call(f32[3,1,2560]{2,1,0:T(1,128)S(1)} %broadcast_in_dim.8.rows_ref), custom_call_target="tpu_custom_call" | custom-call | flops 100000000 | bytes 7077888 | tf_op jit(solution)/shard_map/bias_tiles/pallas_call | solution.py:68
  41.5 21.0 %attend.1 = (bf16[2048,256]{1,0:T(8,128)(2,1)S(1)}, f32[8,2048]{1,0:T(8,128)S(1)}) custom-call(s32[8]{0:T(128)S(1)} %get-tuple-element.217.refs_0_, s32[8]{0:T(128)S(1)} %get-tuple-element.216.refs_1_, s32[8]{0:T(128)S(1)} %fusion.92.refs_2_, bf16[2048,768]{1,0:T(8,128)(2,1)} %copy-done.52, bf16[2048,768]{1,0:T(8,128)(2,1)} %copy-done.52, ...), custom_call_target="tpu_custom_call" | custom-call | flops 20000000000 | bytes 12000000 | tf_op jit(solution)/shard_map/attend/pallas_call | solution.py:134
  65.1 6.5 %collective-permute-done.8 = bf16[512,192]{1,0:T(8,128)(2,1)S(1)} collective-permute-done((bf16[512,192]{1,0:T(8,128)(2,1)S(1)}, bf16[512,192]{1,0:T(8,128)(2,1)S(1)}, u32[]{:S(2)}, u32[]{:S(2)}) %collective-permute-start.8) | collective-permute-done | bytes 196640 | tf_op jit(solution)/shard_map/ppermute | solution.py:458
  71.7 5.8 %collective-permute-done.7 = bf16[512,192]{1,0:T(8,128)(2,1)S(1)} collective-permute-done((bf16[512,192]{1,0:T(8,128)(2,1)S(1)}, bf16[512,192]{1,0:T(8,128)(2,1)S(1)}, u32[]{:S(2)}, u32[]{:S(2)}) %collective-permute-start.7) | collective-permute-done | bytes 196640 | tf_op jit(solution)/shard_map/ppermute | solution.py:458
  83.2 10.4 %all-to-all-start = ((bf16[8,8,16,768]{3,2,1,0:T(8,128)(2,1)}), bf16[8,8,16,768]{3,2,1,0:T(8,128)(2,1)S(1)}, u32[]{:S(2)}, u32[]{:S(2)}) async-start(bf16[8,8,16,768]{3,2,1,0:T(8,128)(2,1)} %bitcast.116), calls=%async_computation | async-start | bytes 3145728 | tf_op jit(solution)/shard_map/all_to_all | solution.py:473
  94.3 36.4 %all-to-all-done = bf16[8,8,16,768]{3,2,1,0:T(8,128)(2,1)S(1)} async-done(((bf16[8,8,16,768]{3,2,1,0:T(8,128)(2,1)}), bf16[8,8,16,768]{3,2,1,0:T(8,128)(2,1)S(1)}, u32[]{:S(2)}, u32[]{:S(2)}) %all-to-all-start) | async-done | bytes 1572896 | tf_op jit(solution)/shard_map/all_to_all | solution.py:473
  132.7 17.2 %collective-permute-done.13.refs_2_ = bf16[8,4,16,768]{3,2,1,0:T(8,128)(2,1)S(1)} collective-permute-done((bf16[8,4,16,768]{3,2,1,0:T(8,128)(2,1)S(1)}, bf16[8,4,16,768]{3,2,1,0:T(8,128)(2,1)S(1)}, u32[]{:S(2)}, u32[]{:S(2)}) %collective-permute-start.13) | collective-permute-done | bytes 786464 | tf_op jit(solution)/shard_map/ppermute | solution.py:458
  153.1 18.5 %experts.2 = (bf16[8,4,16,768]{3,2,1,0:T(8,128)(2,1)S(1)}, bf16[8,4,16,768]{3,2,1,0:T(8,128)(2,1)S(1)}, bf16[8,4,16,768]{3,2,1,0:T(8,128)(2,1)S(1)}, bf16[8,4,16...) custom-call(bf16[8,4,16,768]{3,2,1,0:T(8,128)(2,1)} %copy-done.2, ...), custom_call_target="tpu_custom_call" | custom-call | flops 7247757312 | bytes 28000000 | tf_op jit(solution)/shard_map/experts/pallas_call | solution.py:352
  178.2 18.3 %experts.3 = (bf16[8,4,16,768]{3,2,1,0:T(8,128)(2,1)S(1)}, bf16[8,4,16,768]{3,2,1,0:T(8,128)(2,1)}, bf16[8,4,16,768]{3,2,1,0:T(8,128)(2,1)S(1)}, bf16[8,4,16,768...) custom-call(bf16[8,4,16,768]{3,2,1,0:T(8,128)(2,1)} %get-tuple-eleme, ...), custom_call_target="tpu_custom_call" | custom-call | flops 7247757312 | bytes 28000000 | tf_op jit(solution)/shard_map/experts/pallas_call | solution.py:352
  199.4 17.3 %expert_weights.2 = (bf16[8,8,16,768]{3,2,1,0:T(8,128)(2,1)}, bf16[8,8,16,768]{3,2,1,0:T(8,128)(2,1)}, bf16[8,8,16,768]{3,2,1,0:T(8,128)(2,1)}, bf16[8,8,16,768]...) custom-call(bf16[8,4,16,768]{3,2,1,0:T(8,128)(2,1)} %get-tuple-element.185.refs_0_, ...), custom_call_target="tpu_custom_call" | custom-call | flops 7247757312 | bytes 40000000 | tf_op jit(solution)/shard_map/expert_weights/pallas_call | solution.py:425
  225.2 17.0 %expert_weights.3 = (bf16[8,8,16,768]{3,2,1,0:T(8,128)(2,1)}, bf16[8,8,16,768]{3,2,1,0:T(8,128)(2,1)}, bf16[8,8,16,768]{3,2,1,0:T(8,128)(2,1)}, bf16[8,8,16,768]...) custom-call(bf16[8,4,16,768]{3,2,1,0:T(8,128)(2,1)S(1)} %copy-done.3, ...), custom_call_target="tpu_custom_call", output_to_operand_aliasing={{0}: (9, {}), {1}: (10, {}), {2}: (11, {}), {3}: (12, {}), ... | custom-call | flops 7247757312 | bytes 40000000 | tf_op jit(solution)/shard_map/expert_weights/pallas_call | solution.py:425
  246.3 5.8 %all-to-all-start.2 = ((bf16[8,4,16,768]{3,2,1,0:T(8,128)(2,1)}), bf16[8,4,16,768]{3,2,1,0:T(8,128)(2,1)}, u32[]{:S(2)}, u32[]{:S(2)}) async-start(bf16[8,4,16,768]{3,2,1,0:T(8,128)(2,1)} %add_convert_fusion.5), calls=%async_computation.2 | async-start | bytes 1572864 | tf_op jit(solution)/shard_map/all_to_all | solution.py:473
  263.8 8.7 %all-to-all-done.2 = bf16[8,4,16,768]{3,2,1,0:T(8,128)(2,1)} async-done(((bf16[8,4,16,768]{3,2,1,0:T(8,128)(2,1)}), bf16[8,4,16,768]{3,2,1,0:T(8,128)(2,1)}, u32[]{:S(2)}, u32[]{:S(2)}) %all-to-all-start.2) | async-done | bytes 786464 | tf_op jit(solution)/shard_map/all_to_all | solution.py:473
  287.3 17.0 %collective-permute-done.35 = bf16[512,192]{1,0:T(8,128)(2,1)S(1)} collective-permute-done((bf16[512,192]{1,0:T(8,128)(2,1)S(1)}, bf16[512,192]{1,0:T(8,128)(2,1)S(1)}, u32[]{:S(2)}, u32[]{:S(2)}) %collective-permute-start.35) | collective-permute-done | bytes 196640 | tf_op jit(solution)/shard_map/ppermute | solution.py:458
  318.3 29.4 %attend_back.2 = (bf16[2048,128]{1,0:T(8,128)(2,1)S(1)}, bf16[2048,128]{1,0:T(8,128)(2,1)S(1)}, bf16[2048,128]{1,0:T(8,128)(2,1)S(1)}, f32[8,2560]{1,0:T(8,128)S(1)}) custom-call(s32[8]{0:T(128)S(1)} %get-tuple-element.217.refs_0_, s32[8]{0:T(128)S(1)} %get-tuple-element.216.refs_1_, s32[8]{0:T(128)S(1)} %copy-done.29, bf16[2048,768]{1,0:T(8,128)(2,1)} %copy-done.52, ...), custom_call_target="tpu_custom_call" | custom-call | flops 28000000000 | bytes 10000000 | tf_op jit(solution)/shard_map/attend_back/pallas_call | solution.py:247
  355.1 6.2 %collective-permute-done.40 = f32[768,65]{1,0:T(8,128)} collective-permute-done((f32[768,65]{1,0:T(8,128)}, f32[768,65]{1,0:T(8,128)}, u32[]{:S(2)}, u32[]{:S(2)}) %collective-permute-start.40) | collective-permute-done | bytes 199712 | tf_op jit(solution)/shard_map/ppermute | solution.py:458
  366.5 6.4 %collective-permute-start.25 = (bf16[2,2,8,16,768]{4,3,2,1,0:T(8,128)(2,1)}, bf16[2,2,8,16,768]{4,3,2,1,0:T(8,128)(2,1)}, u32[]{:S(2)}, u32[]{:S(2)}) collective-permute-start(bf16[2,2,8,16,768]{4,3,2,1,0:T(8,128)(2,1)} %broadcast_select_fusion.2), channel_id=1, source_target_pairs={{0,8},{4,12},{8,0},{12,4},{16,24},{20,28},{24,16},{28,20},{1,9},{5... | collective-permute-start | bytes 2359304 | tf_op jit(solution)/shard_map/ppermute | solution.py:458
  377.6 19.3 %attend_back.3 = (bf16[2048,128]{1,0:T(8,128)(2,1)S(1)}, bf16[2048,128]{1,0:T(8,128)(2,1)S(1)}, bf16[2048,128]{1,0:T(8,128)(2,1)S(1)}, f32[8,2560]{1,0:T(8,128)S(1)}) custom-call(s32[8]{0:T(128)S(1)} %get-tuple-element.217.refs_0_, s32[8]{0:T(128)S(1)} %get-tuple-element.216.refs_1_, s32[8]{0:T(128)S(1)} %copy-done.29, bf16[2048,768]{1,0:T(8,128)(2,1)} %copy-done.52, ...), custom_call_target="tpu_custom_call" | custom-call | flops 14000000000 | bytes 5000000 | tf_op jit(solution)/shard_map/attend_back/pallas_call | solution.py:247
  416.3 6.3 %convolution_convert_fusion = bf16[2048,768]{1,0:T(8,128)(2,1)} fusion(bf16[2048,576]{1,0:T(8,128)(2,1)} %concatenate.92, bf16[768,576]{0,1:T(8,128)(2,1)} %get-tuple-element.200), kind=kOutput, calls=%fused_computation.2 | convolution fusion | flops 1813512192 | bytes 6389760 | tf_op jit(solution)/shard_map/dot_general | solution.py:37
  422.5 6.3 %all-to-all-start.4 = ((bf16[8,96,641]{2,1,0:T(8,128)(2,1)}), bf16[8,96,641]{2,1,0:T(8,128)(2,1)S(1)}, u32[]{:S(2)}, u32[]{:S(2)}) async-start(bf16[8,96,641]{2,1,0:T(8,128)(2,1)} %pad_maximum_fusion.4), calls=%async_computation.4 | async-start | bytes 2359296 | tf_op jit(solution)/shard_map/all_to_all | solution.py:473
  433.7 13.2 %collective-permute-done.45 = f32[8,128]{1,0:T(8,128)S(1)} collective-permute-done((f32[8,128]{1,0:T(8,128)S(1)}, f32[8,128]{1,0:T(8,128)S(1)}, u32[]{:S(2)}, u32[]{:S(2)}) %collective-permute-start.45) | collective-permute-done | bytes 4128 | tf_op jit(solution)/shard_map/ppermute | solution.py:458
  472.2 13.1 %collective-permute-done.26 = bf16[4,1,8,16,768]{4,3,2,1,0:T(8,128)(2,1)} collective-permute-done((bf16[4,1,8,16,768]{4,3,2,1,0:T(8,128)(2,1)}, bf16[4,1,8,16,768]{4,3,2,1,0:T(8,128)(2,1)}, u32[]{:S(2)}, u32[]{:S(2)}) %collective-permute-start.26) | collective-permute-done | bytes 786464 | tf_op jit(solution)/shard_map/ppermute | solution.py:458
  496.6 5.6 %all-to-all-done.6 = bf16[8,96,833]{2,1,0:T(8,128)(2,1)S(1)} async-done(((bf16[8,96,833]{2,1,0:T(8,128)(2,1)}), bf16[8,96,833]{2,1,0:T(8,128)(2,1)S(1)}, u32[]{:S(2)}, u32[]{:S(2)}) %all-to-all-start.6) | async-done | bytes 1279520 | tf_op jit(solution)/shard_map/all_to_all | solution.py:473
  (398 shorter events, 183.2 us)
Async XLA Ops:
  4.4 27.5 %collective-permute-start.3 = (bf16[256,768]{1,0:T(8,128)(2,1)S(1)}, bf16[256,768]{1,0:T(8,128)(2,1)S(1)}, u32[]{:S(2)}, u32[]{:S(2)}) collective-permute-start(bf16[256,768]{1,0:T(8,128)(2,1)S(1)} %get-tuple-element.191), channel_id=1, source_target_pairs={{0,2},{1,3},{2,0},{3,1},{4,6},{5,7},{6,4},{7,5},{8,10},{9,11},{10,... | collective-permute-start | bytes 1179656 | tf_op jit(solution)/shard_map/ppermute | solution.py:458
  10.5 72.7 %all-to-all-start.1 = ((bf16[8,8,16,768]{3,2,1,0:T(8,128)(2,1)}), bf16[8,8,16,768]{3,2,1,0:T(8,128)(2,1)}, u32[]{:S(2)}, u32[]{:S(2)}) async-start(bf16[8,8,16,768]{3,2,1,0:T(8,128)(2,1)} %bitcast.10), calls=%async_computation.1 | async-start | bytes 3145728 | tf_op jit(solution)/shard_map/all_to_all | solution.py:473
  34.4 28.2 %collective-permute-start.10 = (bf16[192,768]{1,0:T(8,128)(2,1)S(1)}, bf16[192,768]{1,0:T(8,128)(2,1)}, u32[]{:S(2)}, u32[]{:S(2)}) collective-permute-start(bf16[192,768]{1,0:T(8,128)(2,1)S(1)} %copy-done.57), channel_id=1, source_target_pairs={{0,2},{1,3},{2,0},{3,1},{4,6},{5,7},{6,4},{7,5},{8,10},{9,11},{10,... | collective-permute-start | bytes 884744 | tf_op jit(solution)/shard_map/ppermute | solution.py:458
  36.0 41.6 %collective-permute-start.9 = (bf16[192,768]{1,0:T(8,128)(2,1)S(1)}, bf16[192,768]{1,0:T(8,128)(2,1)}, u32[]{:S(2)}, u32[]{:S(2)}) collective-permute-start(bf16[192,768]{1,0:T(8,128)(2,1)S(1)} %copy-done.57), channel_id=1, source_target_pairs={{0,1},{1,0},{2,3},{3,2},{4,5},{5,4},{6,7},{7,6},{8,9},{9,8},{10,11... | collective-permute-start | bytes 884744 | tf_op jit(solution)/shard_map/ppermute | solution.py:458
  83.2 47.5 %all-to-all-start = ((bf16[8,8,16,768]{3,2,1,0:T(8,128)(2,1)}), bf16[8,8,16,768]{3,2,1,0:T(8,128)(2,1)S(1)}, u32[]{:S(2)}, u32[]{:S(2)}) async-start(bf16[8,8,16,768]{3,2,1,0:T(8,128)(2,1)} %bitcast.116), calls=%async_computation | async-start | bytes 3145728 | tf_op jit(solution)/shard_map/all_to_all | solution.py:473
  93.7 38.5 %collective-permute-start.16 = (bf16[8,8,16,768]{3,2,1,0:T(8,128)(2,1)}, bf16[8,8,16,768]{3,2,1,0:T(8,128)(2,1)}, u32[]{:S(2)}, u32[]{:S(2)}) collective-permute-start(bf16[8,8,16,768]{3,2,1,0:T(8,128)(2,1)} %all-to-all-done.1.refs_4_), channel_id=1, source_target_pairs={{0,2},{1,3},{2,0},{3,1},{4,6},{5,7},{6,4},{7,5},{8,10},{9,11},{10,... | collective-permute-start | bytes 4718600 | tf_op jit(solution)/shard_map/ppermute | solution.py:458
  94.3 56.5 %collective-permute-start.15 = (bf16[8,8,16,768]{3,2,1,0:T(8,128)(2,1)}, bf16[8,8,16,768]{3,2,1,0:T(8,128)(2,1)}, u32[]{:S(2)}, u32[]{:S(2)}) collective-permute-start(bf16[8,8,16,768]{3,2,1,0:T(8,128)(2,1)} %all-to-all-done.1.refs_4_), channel_id=1, source_target_pairs={{0,1},{1,0},{2,3},{3,2},{4,5},{5,4},{6,7},{7,6},{8,9},{9,8},{10,11... | collective-permute-start | bytes 4718600 | tf_op jit(solution)/shard_map/ppermute | solution.py:458
  173.8 42.9 %collective-permute-start.30 = (bf16[8,4,16,768]{3,2,1,0:T(8,128)(2,1)S(1)}, bf16[8,4,16,768]{3,2,1,0:T(8,128)(2,1)S(1)}, u32[]{:S(2)}, u32[]{:S(2)}) collective-permute-start(bf16[8,4,16,768]{3,2,1,0:T(8,128)(2,1)S(1)} %get-tuple-element.85), channel_id=1, source_target_pairs={{0,1},{1,0},{2,3},{3,2},{4,5},{5,4},{6,7},{7,6},{8,9},{9,8},{10,11... | collective-permute-start | bytes 2359304 | tf_op jit(solution)/shard_map/ppermute | solution.py:458
  174.3 42.4 %collective-permute-start.32 = (bf16[8,4,16,768]{3,2,1,0:T(8,128)(2,1)S(1)}, bf16[8,4,16,768]{3,2,1,0:T(8,128)(2,1)S(1)}, u32[]{:S(2)}, u32[]{:S(2)}) collective-permute-start(bf16[8,4,16,768]{3,2,1,0:T(8,128)(2,1)S(1)} %add_convert_fusion.4), channel_id=1, source_target_pairs={{0,2},{1,3},{2,0},{3,1},{4,6},{5,7},{6,4},{7,5},{8,10},{9,11},{10,... | collective-permute-start | bytes 2359304 | tf_op jit(solution)/shard_map/ppermute | solution.py:458
  196.5 46.6 %collective-permute-start.27 = (bf16[8,4,16,768]{3,2,1,0:T(8,128)(2,1)}, bf16[8,4,16,768]{3,2,1,0:T(8,128)(2,1)}, u32[]{:S(2)}, u32[]{:S(2)}) collective-permute-start(bf16[8,4,16,768]{3,2,1,0:T(8,128)(2,1)} %get-tuple-element.81), channel_id=1, source_target_pairs={{0,1},{1,0},{2,3},{3,2},{4,5},{5,4},{6,7},{7,6},{8,9},{9,8},{10,11... | collective-permute-start | bytes 2359304 | tf_op jit(solution)/shard_map/ppermute | solution.py:458
  196.7 26.4 %collective-permute-start.28 = (bf16[8,4,16,768]{3,2,1,0:T(8,128)(2,1)}, bf16[8,4,16,768]{3,2,1,0:T(8,128)(2,1)}, u32[]{:S(2)}, u32[]{:S(2)}) collective-permute-start(bf16[8,4,16,768]{3,2,1,0:T(8,128)(2,1)} %get-tuple-element.83), channel_id=1, source_target_pairs={{0,1},{1,0},{2,3},{3,2},{4,5},{5,4},{6,7},{7,6},{8,9},{9,8},{10,11... | collective-permute-start | bytes 2359304 | tf_op jit(solution)/shard_map/ppermute | solution.py:458
  217.9 28.5 %all-to-all-start.3 = ((bf16[8,4,16,768]{3,2,1,0:T(8,128)(2,1)}), bf16[8,4,16,768]{3,2,1,0:T(8,128)(2,1)}, u32[]{:S(2)}, u32[]{:S(2)}) async-start(bf16[8,4,16,768]{3,2,1,0:T(8,128)(2,1)} %add_convert_fusion.3), calls=%async_computation.3 | async-start | bytes 1572864 | tf_op jit(solution)/shard_map/all_to_all | solution.py:473
  259.0 53.0 %collective-permute-start.21 = (bf16[8,8,16,768]{3,2,1,0:T(8,128)(2,1)}, bf16[8,8,16,768]{3,2,1,0:T(8,128)(2,1)}, u32[]{:S(2)}, u32[]{:S(2)}) collective-permute-start(bf16[8,8,16,768]{3,2,1,0:T(8,128)(2,1)} %get-tuple-element.77), channel_id=1, source_target_pairs={{0,1},{1,0},{2,3},{3,2},{4,5},{5,4},{6,7},{7,6},{8,9},{9,8},{10,11... | collective-permute-start | bytes 4718600 | tf_op jit(solution)/shard_map/ppermute | solution.py:458
  262.9 49.2 %collective-permute-start.23 = (bf16[8,8,16,768]{3,2,1,0:T(8,128)(2,1)}, bf16[8,8,16,768]{3,2,1,0:T(8,128)(2,1)}, u32[]{:S(2)}, u32[]{:S(2)}) collective-permute-start(bf16[8,8,16,768]{3,2,1,0:T(8,128)(2,1)} %add_convert_fusion.1.refs_13_), channel_id=1, source_target_pairs={{0,2},{1,3},{2,0},{3,1},{4,6},{5,7},{6,4},{7,5},{8,10},{9,11},{10,... | collective-permute-start | bytes 4718600 | tf_op jit(solution)/shard_map/ppermute | solution.py:458
  304.3 43.4 %collective-permute-start.39 = (f32[768,65]{1,0:T(8,128)}, f32[768,65]{1,0:T(8,128)S(1)}, u32[]{:S(2)}, u32[]{:S(2)}) collective-permute-start(f32[768,65]{1,0:T(8,128)} %pad_maximum_fusion.8), channel_id=1, source_target_pairs={{0,1},{1,0},{2,3},{3,2},{4,5},{5,4},{6,7},{7,6},{8,9},{9,8},{10,11... | collective-permute-start | bytes 599048 | tf_op jit(solution)/shard_map/ppermute | solution.py:458
  310.7 44.4 %collective-permute-start.37 = (bf16[512,768]{1,0:T(8,128)(2,1)}, bf16[512,768]{1,0:T(8,128)(2,1)}, u32[]{:S(2)}, u32[]{:S(2)}) collective-permute-start(bf16[512,768]{1,0:T(8,128)(2,1)} %fusion.103), channel_id=1, source_target_pairs={{0,2},{1,3},{2,0},{3,1},{4,6},{5,7},{6,4},{7,5},{8,10},{9,11},{10,... | collective-permute-start | bytes 2359304 | tf_op jit(solution)/shard_map/ppermute | solution.py:458
  312.1 60.9 %collective-permute-start.36 = (bf16[512,768]{1,0:T(8,128)(2,1)}, bf16[512,768]{1,0:T(8,128)(2,1)}, u32[]{:S(2)}, u32[]{:S(2)}) collective-permute-start(bf16[512,768]{1,0:T(8,128)(2,1)} %fusion.103), channel_id=1, source_target_pairs={{0,1},{1,0},{2,3},{3,2},{4,5},{5,4},{6,7},{7,6},{8,9},{9,8},{10,11... | collective-permute-start | bytes 2359304 | tf_op jit(solution)/shard_map/ppermute | solution.py:458
  315.6 46.8 %collective-permute-start.24 = (bf16[1,4,8,16,768]{4,3,2,1,0:T(8,128)(2,1)}, bf16[1,4,8,16,768]{4,3,2,1,0:T(8,128)(2,1)}, u32[]{:S(2)}, u32[]{:S(2)}) collective-permute-start(bf16[1,4,8,16,768]{4,3,2,1,0:T(8,128)(2,1)} %broadcast_select_fusion), channel_id=1, source_target_pairs={{0,16},{4,20},{8,24},{12,28},{16,0},{20,4},{24,8},{28,12},{1,17},{... | collective-permute-start | bytes 2359304 | tf_op jit(solution)/shard_map/ppermute | solution.py:458
  366.5 62.4 %collective-permute-start.25 = (bf16[2,2,8,16,768]{4,3,2,1,0:T(8,128)(2,1)}, bf16[2,2,8,16,768]{4,3,2,1,0:T(8,128)(2,1)}, u32[]{:S(2)}, u32[]{:S(2)}) collective-permute-start(bf16[2,2,8,16,768]{4,3,2,1,0:T(8,128)(2,1)} %broadcast_select_fusion.2), channel_id=1, source_target_pairs={{0,8},{4,12},{8,0},{12,4},{16,24},{20,28},{24,16},{28,20},{1,9},{5... | collective-permute-start | bytes 2359304 | tf_op jit(solution)/shard_map/ppermute | solution.py:458
  398.7 31.6 %collective-permute-start.44 = (f32[8,128]{1,0:T(8,128)S(1)}, f32[8,128]{1,0:T(8,128)S(1)}, u32[]{:S(2)}, u32[]{:S(2)}) collective-permute-start(f32[8,128]{1,0:T(8,128)S(1)} %fusion.89), channel_id=1, source_target_pairs={{0,4},{4,0},{8,12},{12,8},{16,20},{20,16},{24,28},{28,24},{1,5},{5... | collective-permute-start | bytes 12296 | tf_op jit(solution)/shard_map/ppermute | solution.py:458
  422.5 41.9 %all-to-all-start.4 = ((bf16[8,96,641]{2,1,0:T(8,128)(2,1)}), bf16[8,96,641]{2,1,0:T(8,128)(2,1)S(1)}, u32[]{:S(2)}, u32[]{:S(2)}) async-start(bf16[8,96,641]{2,1,0:T(8,128)(2,1)} %pad_maximum_fusion.4), calls=%async_computation.4 | async-start | bytes 2359296 | tf_op jit(solution)/shard_map/all_to_all | solution.py:473
  457.5 27.8 %collective-permute-start.26 = (bf16[4,1,8,16,768]{4,3,2,1,0:T(8,128)(2,1)}, bf16[4,1,8,16,768]{4,3,2,1,0:T(8,128)(2,1)}, u32[]{:S(2)}, u32[]{:S(2)}) collective-permute-start(bf16[4,1,8,16,768]{4,3,2,1,0:T(8,128)(2,1)} %bitcast_select_fusion.1), channel_id=1, source_target_pairs={{0,4},{4,0},{8,12},{12,8},{16,20},{20,16},{24,28},{28,24},{1,5},{5... | collective-permute-start | bytes 2359304 | tf_op jit(solution)/shard_map/ppermute | solution.py:458
  458.7 32.6 %collective-permute-start.41 = (bf16[512,768]{1,0:T(8,128)(2,1)}, bf16[512,768]{1,0:T(8,128)(2,1)}, u32[]{:S(2)}, u32[]{:S(2)}) collective-permute-start(bf16[512,768]{1,0:T(8,128)(2,1)} %get-tuple-element.170), channel_id=1, source_target_pairs={{0,1},{1,0},{2,3},{3,2},{4,5},{5,4},{6,7},{7,6},{8,9},{9,8},{10,11... | collective-permute-start | bytes 2359304 | tf_op jit(solution)/shard_map/ppermute | solution.py:458
  466.0 36.3 %all-to-all-start.6 = ((bf16[8,96,833]{2,1,0:T(8,128)(2,1)}), bf16[8,96,833]{2,1,0:T(8,128)(2,1)S(1)}, u32[]{:S(2)}, u32[]{:S(2)}) async-start(bf16[8,96,833]{2,1,0:T(8,128)(2,1)} %broadcast_in_dim.11), calls=%async_computation.6 | async-start | bytes 2752512 | tf_op jit(solution)/shard_map/all_to_all | solution.py:473
  (116 other events, 1199.7 us)
where the time goes:
time: 518 us; the launch traced here: 510 us
  Pallas kernels  153 us (30%)
  waiting for transfers between devices  146 us (28%)
  starting transfers between devices  86 us (17%)
  other arithmetic  44.8 us (9%)
  local copies, waits for them, and re-layouts  44.5 us (9%)
  matrix products  32.9 us (6%)
    ppermute x49, waiting for transfers between devices, swap(): return lax.ppermute(values, axis, [(n, n ^ step) for n in range(count)])  95.5 us
    all_to_all x7, waiting for transfers between devices, trade_dp(): return lax.all_to_all(values, 'dp', split_axis=0, concat_axis=0, tiled=True)  50.7 us
    pallas_call x2, Pallas kernels, attend_back(): pl.pallas_call(lambda *refs: attend_back_kernel(count, head_dim, reach, f...  48.6 us
    ppermute x49, starting transfers between devices, swap(): return lax.ppermute(values, axis, [(n, n ^ step) for n in range(count)])  44.1 us
    all_to_all x7, starting transfers between devices, trade_dp(): return lax.all_to_all(values, 'dp', split_axis=0, concat_axis=0, tiled=True)  41.9 us
    pallas_call x2, Pallas kernels, experts(): pl.pallas_call(lambda *refs: expert_kernel(groups, *refs), out_shape=[jax...  36.8 us
    pallas_call x2, Pallas kernels, expert_weights(): pl.pallas_call(lambda *refs: weight_kernel(groups, *refs), out_shape=[jax...  34.3 us
    pallas_call x1, Pallas kernels, attend(): pl.pallas_call(lambda *refs: attend_kernel(heads, head_dim, reach, *refs)...  21 us
  transfers between devices with their start and end apart: 56, of which 17 were waited for; matrix products, arithmetic and copies ran while one was open for 20% of the time, Pallas kernels for 30%

commit v1 on v0

--- a/solution.py
+++ b/solution.py
@@ -469,6 +469,10 @@
     return near + swap(far.astype(BF16), "mp", 2).astype(F32)
 
 
+def unless_nan(values, flag):
+    return jnp.where(flag != flag, jnp.zeros_like(values), values)
+
+
 def trade_dp(values):
     return lax.all_to_all(values, "dp", split_axis=0, concat_axis=0, tiled=True)
 
@@ -673,12 +677,15 @@
             seg_row, spans, ready,
         )
         lanes = min(LANES, head_width - g * LANES)
-        own = jnp.concatenate([grad_q[:, :lanes], grad_k[:, :lanes], grad_v[:, :lanes]], axis=1)
-        weights = jnp.concatenate([w[:, g * LANES : g * LANES + lanes] for w in padded], axis=1)
+        own = jnp.concatenate([grad_q, grad_k, grad_v], axis=1)
+        weights = jnp.concatenate([w[:, g * LANES : (g + 1) * LANES] for w in padded], axis=1)
         order.append((own, weights))
         partial = dot_tn(normed_all, own)
         gain_sum = gain_sum + jnp.sum(partial * weights.astype(F32), axis=1)
-        payload = jnp.concatenate([partial] + rest, axis=1).astype(BF16)
+        partial = [partial[:, n * LANES : n * LANES + lanes] for n in range(3)]
+        payload = jnp.concatenate(partial + rest, axis=1).astype(BF16)
+        if summed:
+            payload = unless_nan(payload, summed[-1][0, 0])
         piece_of.append((lanes, payload.shape[1]))
         rest, ready = [], [payload, folded_rows]
         summed.append(fold_dp(payload))

time: 518 us -> 506 us (0.977)
    ppermute x49, waiting for transfers between devices: 95.5 us -> 85.3 us  [swap(): return lax.ppermute(values, axis, [(n, n ^ step) for n in range(count)])]
    all_to_all x7, waiting for transfers between devices: 50.7 us -> 58.6 us  [trade_dp(): return lax.all_to_all(values, 'dp', split_axis=0, concat_axis=0, tiled=True)]
    unnamed x182 -> x176, local copies, waits for them, and re-layouts: 17.9 us -> 22.2 us
  transfers between devices with their start and end apart: 56 -> 56, of which waited for: 17 -> 20; matrix products, arithmetic and copies ran while one was open for 20% -> 18% of each run, Pallas kernels for 30% -> 31%
where the time goes in v1:
time: 506 us; the launch traced here: 498 us
  Pallas kernels  152 us (30%)
  waiting for transfers between devices  144 us (28%)
  starting transfers between devices  82.3 us (16%)
  other arithmetic  42.3 us (8%)
  local copies, waits for them, and re-layouts  41.4 us (8%)
  matrix products  32 us (6%)
    ppermute x49, waiting for transfers between devices, swap(): return lax.ppermute(values, axis, [(n, n ^ step) for n in range(count)])  85.3 us
    all_to_all x7, waiting for transfers between devices, trade_dp(): return lax.all_to_all(values, 'dp', split_axis=0, concat_axis=0, tiled=True)  58.6 us
    pallas_call x2, Pallas kernels, attend_back(): pl.pallas_call(lambda *refs: attend_back_kernel(count, head_dim, reach, f...  48.3 us
    ppermute x49, starting transfers between devices, swap(): return lax.ppermute(values, axis, [(n, n ^ step) for n in range(count)])  41.3 us
    all_to_all x7, starting transfers between devices, trade_dp(): return lax.all_to_all(values, 'dp', split_axis=0, concat_axis=0, tiled=True)  41 us
    pallas_call x2, Pallas kernels, experts(): pl.pallas_call(lambda *refs: expert_kernel(groups, *refs), out_shape=[jax...  36.7 us
    pallas_call x2, Pallas kernels, expert_weights(): pl.pallas_call(lambda *refs: weight_kernel(groups, *refs), out_shape=[jax...  34.3 us
    unnamed x176, local copies, waits for them, and re-layouts  22.2 us
  transfers between devices with their start and end apart: 56, of which 20 were waited for; matrix products, arithmetic and copies ran while one was open for 18% of the time, Pallas kernels for 31%

profile of v1, /device:TPU:0, one launch (start us, length us, event | category | flops | bytes accessed | tf_op | source)
XLA Modules:
  0.0 498.0 jit_solution(5074297406437096771)
XLA Ops:
  11.3 6.2 %all-to-all-start.1 = ((bf16[8,8,16,768]{3,2,1,0:T(8,128)(2,1)}), bf16[8,8,16,768]{3,2,1,0:T(8,128)(2,1)}, u32[]{:S(2)}, u32[]{:S(2)}) async-start(bf16[8,8,16,768]{3,2,1,0:T(8,128)(2,1)} %bitcast.10), calls=%async_computation.1 | async-start | bytes 3145728 | tf_op jit(solution)/shard_map/all_to_all | solution.py:477
  21.0 11.9 %bias_tiles.1.refs_6_.refs_10_ = f32[3,9,256,256]{3,2,1,0:T(8,128)} custom-call(f32[3,1,2560]{2,1,0:T(1,128)S(1)} %broadcast_in_dim.10.rows_ref), custom_call_target="tpu_custom_call" | custom-call | flops 100000000 | bytes 7077888 | tf_op jit(solution)/shard_map/bias_tiles/pallas_call | solution.py:68
  42.4 21.0 %attend.1 = (bf16[2048,256]{1,0:T(8,128)(2,1)S(1)}, f32[8,2048]{1,0:T(8,128)S(1)}) custom-call(s32[8]{0:T(128)S(1)} %get-tuple-element.217.refs_0_, s32[8]{0:T(128)S(1)} %get-tuple-element.216.refs_1_, s32[8]{0:T(128)S(1)} %fusion.82.refs_2_, bf16[2048,768]{1,0:T(8,128)(2,1)} %copy-done.54, bf16[2048,768]{1,0:T(8,128)(2,1)} %copy-done.54, ...), custom_call_target="tpu_custom_call" | custom-call | flops 20000000000 | bytes 12000000 | tf_op jit(solution)/shard_map/attend/pallas_call | solution.py:134
  66.1 6.5 %collective-permute-done.8 = bf16[512,192]{1,0:T(8,128)(2,1)S(1)} collective-permute-done((bf16[512,192]{1,0:T(8,128)(2,1)S(1)}, bf16[512,192]{1,0:T(8,128)(2,1)S(1)}, u32[]{:S(2)}, u32[]{:S(2)}) %collective-permute-start.8) | collective-permute-done | bytes 196640 | tf_op jit(solution)/shard_map/ppermute | solution.py:458
  72.6 5.8 %collective-permute-done.7 = bf16[512,192]{1,0:T(8,128)(2,1)S(1)} collective-permute-done((bf16[512,192]{1,0:T(8,128)(2,1)S(1)}, bf16[512,192]{1,0:T(8,128)(2,1)S(1)}, u32[]{:S(2)}, u32[]{:S(2)}) %collective-permute-start.7) | collective-permute-done | bytes 196640 | tf_op jit(solution)/shard_map/ppermute | solution.py:458
  84.3 11.3 %all-to-all-start = ((bf16[8,8,16,768]{3,2,1,0:T(8,128)(2,1)}), bf16[8,8,16,768]{3,2,1,0:T(8,128)(2,1)S(1)}, u32[]{:S(2)}, u32[]{:S(2)}) async-start(bf16[8,8,16,768]{3,2,1,0:T(8,128)(2,1)} %bitcast.112), calls=%async_computation | async-start | bytes 3145728 | tf_op jit(solution)/shard_map/all_to_all | solution.py:477
  96.3 36.4 %all-to-all-done = bf16[8,8,16,768]{3,2,1,0:T(8,128)(2,1)S(1)} async-done(((bf16[8,8,16,768]{3,2,1,0:T(8,128)(2,1)}), bf16[8,8,16,768]{3,2,1,0:T(8,128)(2,1)S(1)}, u32[]{:S(2)}, u32[]{:S(2)}) %all-to-all-start) | async-done | bytes 1572896 | tf_op jit(solution)/shard_map/all_to_all | solution.py:477
  134.7 17.2 %collective-permute-done.13.refs_2_ = bf16[8,4,16,768]{3,2,1,0:T(8,128)(2,1)S(1)} collective-permute-done((bf16[8,4,16,768]{3,2,1,0:T(8,128)(2,1)S(1)}, bf16[8,4,16,768]{3,2,1,0:T(8,128)(2,1)S(1)}, u32[]{:S(2)}, u32[]{:S(2)}) %collective-permute-start.13) | collective-permute-done | bytes 786464 | tf_op jit(solution)/shard_map/ppermute | solution.py:458
  155.1 18.4 %experts.2 = (bf16[8,4,16,768]{3,2,1,0:T(8,128)(2,1)S(1)}, bf16[8,4,16,768]{3,2,1,0:T(8,128)(2,1)S(1)}, bf16[8,4,16,768]{3,2,1,0:T(8,128)(2,1)S(1)}, bf16[8,4,16...) custom-call(bf16[8,4,16,768]{3,2,1,0:T(8,128)(2,1)} %copy-done.2, ...), custom_call_target="tpu_custom_call" | custom-call | flops 7247757312 | bytes 28000000 | tf_op jit(solution)/shard_map/experts/pallas_call | solution.py:352
  180.0 18.3 %experts.3 = (bf16[8,4,16,768]{3,2,1,0:T(8,128)(2,1)S(1)}, bf16[8,4,16,768]{3,2,1,0:T(8,128)(2,1)}, bf16[8,4,16,768]{3,2,1,0:T(8,128)(2,1)S(1)}, bf16[8,4,16,768...) custom-call(bf16[8,4,16,768]{3,2,1,0:T(8,128)(2,1)} %get-tuple-eleme, ...), custom_call_target="tpu_custom_call" | custom-call | flops 7247757312 | bytes 28000000 | tf_op jit(solution)/shard_map/experts/pallas_call | solution.py:352
  201.2 17.3 %expert_weights.2 = (bf16[8,8,16,768]{3,2,1,0:T(8,128)(2,1)}, bf16[8,8,16,768]{3,2,1,0:T(8,128)(2,1)}, bf16[8,8,16,768]{3,2,1,0:T(8,128)(2,1)}, bf16[8,8,16,768]...) custom-call(bf16[8,4,16,768]{3,2,1,0:T(8,128)(2,1)} %get-tuple-element.185.refs_0_, ...), custom_call_target="tpu_custom_call" | custom-call | flops 7247757312 | bytes 40000000 | tf_op jit(solution)/shard_map/expert_weights/pallas_call | solution.py:425
  219.7 5.2 %all-to-all-start.3 = ((bf16[8,4,16,768]{3,2,1,0:T(8,128)(2,1)}), bf16[8,4,16,768]{3,2,1,0:T(8,128)(2,1)}, u32[]{:S(2)}, u32[]{:S(2)}) async-start(bf16[8,4,16,768]{3,2,1,0:T(8,128)(2,1)} %add_convert_fusion.3), calls=%async_computation.3 | async-start | bytes 1572864 | tf_op jit(solution)/shard_map/all_to_all | solution.py:477
  227.1 17.0 %expert_weights.3 = (bf16[8,8,16,768]{3,2,1,0:T(8,128)(2,1)}, bf16[8,8,16,768]{3,2,1,0:T(8,128)(2,1)}, bf16[8,8,16,768]{3,2,1,0:T(8,128)(2,1)}, bf16[8,8,16,768]...) custom-call(bf16[8,4,16,768]{3,2,1,0:T(8,128)(2,1)S(1)} %copy-done.3, ...), custom_call_target="tpu_custom_call", output_to_operand_aliasing={{0}: (9, {}), {1}: (10, {}), {2}: (11, {}), {3}: (12, {}), ... | custom-call | flops 7247757312 | bytes 40000000 | tf_op jit(solution)/shard_map/expert_weights/pallas_call | solution.py:425
  248.2 5.9 %all-to-all-start.2 = ((bf16[8,4,16,768]{3,2,1,0:T(8,128)(2,1)}), bf16[8,4,16,768]{3,2,1,0:T(8,128)(2,1)}, u32[]{:S(2)}, u32[]{:S(2)}) async-start(bf16[8,4,16,768]{3,2,1,0:T(8,128)(2,1)} %add_convert_fusion.5), calls=%async_computation.2 | async-start | bytes 1572864 | tf_op jit(solution)/shard_map/all_to_all | solution.py:477
  264.3 10.0 %all-to-all-done.2 = bf16[8,4,16,768]{3,2,1,0:T(8,128)(2,1)} async-done(((bf16[8,4,16,768]{3,2,1,0:T(8,128)(2,1)}), bf16[8,4,16,768]{3,2,1,0:T(8,128)(2,1)}, u32[]{:S(2)}, u32[]{:S(2)}) %all-to-all-start.2) | async-done | bytes 786464 | tf_op jit(solution)/shard_map/all_to_all | solution.py:477
  289.2 15.7 %collective-permute-done.35 = bf16[512,192]{1,0:T(8,128)(2,1)S(1)} collective-permute-done((bf16[512,192]{1,0:T(8,128)(2,1)S(1)}, bf16[512,192]{1,0:T(8,128)(2,1)S(1)}, u32[]{:S(2)}, u32[]{:S(2)}) %collective-permute-start.35) | collective-permute-done | bytes 196640 | tf_op jit(solution)/shard_map/ppermute | solution.py:458
  318.9 29.4 %attend_back.2 = (bf16[2048,128]{1,0:T(8,128)(2,1)S(1)}, bf16[2048,128]{1,0:T(8,128)(2,1)S(1)}, bf16[2048,128]{1,0:T(8,128)(2,1)S(1)}, f32[8,2560]{1,0:T(8,128)S(1)}) custom-call(s32[8]{0:T(128)S(1)} %get-tuple-element.217.refs_0_, s32[8]{0:T(128)S(1)} %get-tuple-element.216.refs_1_, s32[8]{0:T(128)S(1)} %copy-done.23, bf16[2048,768]{1,0:T(8,128)(2,1)} %copy-done.54, ...), custom_call_target="tpu_custom_call" | custom-call | flops 28000000000 | bytes 10000000 | tf_op jit(solution)/shard_map/attend_back/pallas_call | solution.py:247
  357.8 9.2 %collective-permute-done.40 = f32[768,65]{1,0:T(8,128)S(1)} collective-permute-done((f32[768,65]{1,0:T(8,128)S(1)}, f32[768,65]{1,0:T(8,128)S(1)}, u32[]{:S(2)}, u32[]{:S(2)}) %collective-permute-start.40) | collective-permute-done | bytes 199712 | tf_op jit(solution)/shard_map/ppermute | solution.py:458
  370.7 6.4 %collective-permute-start.25 = (bf16[2,2,8,16,768]{4,3,2,1,0:T(8,128)(2,1)}, bf16[2,2,8,16,768]{4,3,2,1,0:T(8,128)(2,1)}, u32[]{:S(2)}, u32[]{:S(2)}) collective-permute-start(bf16[2,2,8,16,768]{4,3,2,1,0:T(8,128)(2,1)} %broadcast_select_fusion.2), channel_id=1, source_target_pairs={{0,8},{4,12},{8,0},{12,4},{16,24},{20,28},{24,16},{28,20},{1,9},{5... | collective-permute-start | bytes 2359304 | tf_op jit(solution)/shard_map/ppermute | solution.py:458
  386.7 18.9 %attend_back.3 = (bf16[2048,128]{1,0:T(8,128)(2,1)S(1)}, bf16[2048,128]{1,0:T(8,128)(2,1)S(1)}, bf16[2048,128]{1,0:T(8,128)(2,1)S(1)}, f32[8,2560]{1,0:T(8,128)S(1)}) custom-call(s32[8]{0:T(128)S(1)} %get-tuple-element.217.refs_0_, s32[8]{0:T(128)S(1)} %get-tuple-element.216.refs_1_, s32[8]{0:T(128)S(1)} %copy-done.23, bf16[2048,768]{1,0:T(8,128)(2,1)} %copy-done.54, ...), custom_call_target="tpu_custom_call" | custom-call | flops 14000000000 | bytes 5000000 | tf_op jit(solution)/shard_map/attend_back/pallas_call | solution.py:247
  410.6 5.8 %collective-permute-start.44 = (f32[8,128]{1,0:T(8,128)S(1)}, f32[8,128]{1,0:T(8,128)S(1)}, u32[]{:S(2)}, u32[]{:S(2)}) collective-permute-start(f32[8,128]{1,0:T(8,128)S(1)} %fusion.81), channel_id=1, source_target_pairs={{0,4},{4,0},{8,12},{12,8},{16,20},{20,16},{24,28},{28,24},{1,5},{5... | collective-permute-start | bytes 12296 | tf_op jit(solution)/shard_map/ppermute | solution.py:458
  447.2 5.0 %all-to-all-done.5 = bf16[8,96,192]{1,2,0:T(8,128)(2,1)S(1)} async-done(((bf16[8,96,192]{1,2,0:T(8,128)(2,1)}), bf16[8,96,192]{1,2,0:T(8,128)(2,1)S(1)}, u32[]{:S(2)}, u32[]{:S(2)}) %all-to-all-start.5) | async-done | bytes 294944 | tf_op jit(solution)/shard_map/all_to_all | solution.py:477
  460.4 10.2 %collective-permute-done.26 = bf16[4,1,8,16,768]{4,3,2,1,0:T(8,128)(2,1)} collective-permute-done((bf16[4,1,8,16,768]{4,3,2,1,0:T(8,128)(2,1)}, bf16[4,1,8,16,768]{4,3,2,1,0:T(8,128)(2,1)}, u32[]{:S(2)}, u32[]{:S(2)}) %collective-permute-start.26) | collective-permute-done | bytes 786464 | tf_op jit(solution)/shard_map/ppermute | solution.py:458
  483.4 7.2 %all-to-all-done.6 = bf16[8,96,833]{2,1,0:T(8,128)(2,1)S(1)} async-done(((bf16[8,96,833]{2,1,0:T(8,128)(2,1)}), bf16[8,96,833]{2,1,0:T(8,128)(2,1)S(1)}, u32[]{:S(2)}, u32[]{:S(2)}) %all-to-all-start.6) | async-done | bytes 1279520 | tf_op jit(solution)/shard_map/all_to_all | solution.py:477
  (399 shorter events, 177.6 us)
Async XLA Ops:
  5.3 27.6 %collective-permute-start.3 = (bf16[256,768]{1,0:T(8,128)(2,1)}, bf16[256,768]{1,0:T(8,128)(2,1)S(1)}, u32[]{:S(2)}, u32[]{:S(2)}) collective-permute-start(bf16[256,768]{1,0:T(8,128)(2,1)} %get-tuple-element.193), channel_id=1, source_target_pairs={{0,2},{1,3},{2,0},{3,1},{4,6},{5,7},{6,4},{7,5},{8,10},{9,11},{10,... | collective-permute-start | bytes 1179656 | tf_op jit(solution)/shard_map/ppermute | solution.py:458
  11.3 73.0 %all-to-all-start.1 = ((bf16[8,8,16,768]{3,2,1,0:T(8,128)(2,1)}), bf16[8,8,16,768]{3,2,1,0:T(8,128)(2,1)}, u32[]{:S(2)}, u32[]{:S(2)}) async-start(bf16[8,8,16,768]{3,2,1,0:T(8,128)(2,1)} %bitcast.10), calls=%async_computation.1 | async-start | bytes 3145728 | tf_op jit(solution)/shard_map/all_to_all | solution.py:477
  35.4 28.2 %collective-permute-start.10 = (bf16[192,768]{1,0:T(8,128)(2,1)}, bf16[192,768]{1,0:T(8,128)(2,1)}, u32[]{:S(2)}, u32[]{:S(2)}) collective-permute-start(bf16[192,768]{1,0:T(8,128)(2,1)} %param.21), channel_id=1, source_target_pairs={{0,2},{1,3},{2,0},{3,1},{4,6},{5,7},{6,4},{7,5},{8,10},{9,11},{10,... | collective-permute-start | bytes 884744 | tf_op jit(solution)/shard_map/ppermute | solution.py:458
  36.9 41.6 %collective-permute-start.9 = (bf16[192,768]{1,0:T(8,128)(2,1)}, bf16[192,768]{1,0:T(8,128)(2,1)}, u32[]{:S(2)}, u32[]{:S(2)}) collective-permute-start(bf16[192,768]{1,0:T(8,128)(2,1)} %param.21), channel_id=1, source_target_pairs={{0,1},{1,0},{2,3},{3,2},{4,5},{5,4},{6,7},{7,6},{8,9},{9,8},{10,11... | collective-permute-start | bytes 884744 | tf_op jit(solution)/shard_map/ppermute | solution.py:458
  84.3 48.3 %all-to-all-start = ((bf16[8,8,16,768]{3,2,1,0:T(8,128)(2,1)}), bf16[8,8,16,768]{3,2,1,0:T(8,128)(2,1)S(1)}, u32[]{:S(2)}, u32[]{:S(2)}) async-start(bf16[8,8,16,768]{3,2,1,0:T(8,128)(2,1)} %bitcast.112), calls=%async_computation | async-start | bytes 3145728 | tf_op jit(solution)/shard_map/all_to_all | solution.py:477
  95.6 38.6 %collective-permute-start.16 = (bf16[8,8,16,768]{3,2,1,0:T(8,128)(2,1)}, bf16[8,8,16,768]{3,2,1,0:T(8,128)(2,1)}, u32[]{:S(2)}, u32[]{:S(2)}) collective-permute-start(bf16[8,8,16,768]{3,2,1,0:T(8,128)(2,1)} %all-to-all-done.1.refs_4_), channel_id=1, source_target_pairs={{0,2},{1,3},{2,0},{3,1},{4,6},{5,7},{6,4},{7,5},{8,10},{9,11},{10,... | collective-permute-start | bytes 4718600 | tf_op jit(solution)/shard_map/ppermute | solution.py:458
  96.2 56.5 %collective-permute-start.15 = (bf16[8,8,16,768]{3,2,1,0:T(8,128)(2,1)}, bf16[8,8,16,768]{3,2,1,0:T(8,128)(2,1)}, u32[]{:S(2)}, u32[]{:S(2)}) collective-permute-start(bf16[8,8,16,768]{3,2,1,0:T(8,128)(2,1)} %all-to-all-done.1.refs_4_), channel_id=1, source_target_pairs={{0,1},{1,0},{2,3},{3,2},{4,5},{5,4},{6,7},{7,6},{8,9},{9,8},{10,11... | collective-permute-start | bytes 4718600 | tf_op jit(solution)/shard_map/ppermute | solution.py:458
  174.3 44.3 %collective-permute-start.30 = (bf16[8,4,16,768]{3,2,1,0:T(8,128)(2,1)S(1)}, bf16[8,4,16,768]{3,2,1,0:T(8,128)(2,1)S(1)}, u32[]{:S(2)}, u32[]{:S(2)}) collective-permute-start(bf16[8,4,16,768]{3,2,1,0:T(8,128)(2,1)S(1)} %get-tuple-element.85), channel_id=1, source_target_pairs={{0,1},{1,0},{2,3},{3,2},{4,5},{5,4},{6,7},{7,6},{8,9},{9,8},{10,11... | collective-permute-start | bytes 2359304 | tf_op jit(solution)/shard_map/ppermute | solution.py:458
  176.0 42.5 %collective-permute-start.32 = (bf16[8,4,16,768]{3,2,1,0:T(8,128)(2,1)S(1)}, bf16[8,4,16,768]{3,2,1,0:T(8,128)(2,1)S(1)}, u32[]{:S(2)}, u32[]{:S(2)}) collective-permute-start(bf16[8,4,16,768]{3,2,1,0:T(8,128)(2,1)S(1)} %add_convert_fusion.4), channel_id=1, source_target_pairs={{0,2},{1,3},{2,0},{3,1},{4,6},{5,7},{6,4},{7,5},{8,10},{9,11},{10,... | collective-permute-start | bytes 2359304 | tf_op jit(solution)/shard_map/ppermute | solution.py:458
  198.4 46.5 %collective-permute-start.27 = (bf16[8,4,16,768]{3,2,1,0:T(8,128)(2,1)}, bf16[8,4,16,768]{3,2,1,0:T(8,128)(2,1)}, u32[]{:S(2)}, u32[]{:S(2)}) collective-permute-start(bf16[8,4,16,768]{3,2,1,0:T(8,128)(2,1)} %get-tuple-element.81), channel_id=1, source_target_pairs={{0,1},{1,0},{2,3},{3,2},{4,5},{5,4},{6,7},{7,6},{8,9},{9,8},{10,11... | collective-permute-start | bytes 2359304 | tf_op jit(solution)/shard_map/ppermute | solution.py:458
  198.6 26.4 %collective-permute-start.28 = (bf16[8,4,16,768]{3,2,1,0:T(8,128)(2,1)}, bf16[8,4,16,768]{3,2,1,0:T(8,128)(2,1)}, u32[]{:S(2)}, u32[]{:S(2)}) collective-permute-start(bf16[8,4,16,768]{3,2,1,0:T(8,128)(2,1)} %get-tuple-element.83), channel_id=1, source_target_pairs={{0,1},{1,0},{2,3},{3,2},{4,5},{5,4},{6,7},{7,6},{8,9},{9,8},{10,11... | collective-permute-start | bytes 2359304 | tf_op jit(solution)/shard_map/ppermute | solution.py:458
  219.7 28.5 %all-to-all-start.3 = ((bf16[8,4,16,768]{3,2,1,0:T(8,128)(2,1)}), bf16[8,4,16,768]{3,2,1,0:T(8,128)(2,1)}, u32[]{:S(2)}, u32[]{:S(2)}) async-start(bf16[8,4,16,768]{3,2,1,0:T(8,128)(2,1)} %add_convert_fusion.3), calls=%async_computation.3 | async-start | bytes 1572864 | tf_op jit(solution)/shard_map/all_to_all | solution.py:477
  259.7 52.9 %collective-permute-start.21 = (bf16[8,8,16,768]{3,2,1,0:T(8,128)(2,1)}, bf16[8,8,16,768]{3,2,1,0:T(8,128)(2,1)}, u32[]{:S(2)}, u32[]{:S(2)}) collective-permute-start(bf16[8,8,16,768]{3,2,1,0:T(8,128)(2,1)} %get-tuple-element.77), channel_id=1, source_target_pairs={{0,1},{1,0},{2,3},{3,2},{4,5},{5,4},{6,7},{7,6},{8,9},{9,8},{10,11... | collective-permute-start | bytes 4718600 | tf_op jit(solution)/shard_map/ppermute | solution.py:458
  263.5 49.1 %collective-permute-start.23 = (bf16[8,8,16,768]{3,2,1,0:T(8,128)(2,1)}, bf16[8,8,16,768]{3,2,1,0:T(8,128)(2,1)}, u32[]{:S(2)}, u32[]{:S(2)}) collective-permute-start(bf16[8,8,16,768]{3,2,1,0:T(8,128)(2,1)} %add_convert_fusion.1.refs_13_), channel_id=1, source_target_pairs={{0,2},{1,3},{2,0},{3,1},{4,6},{5,7},{6,4},{7,5},{8,10},{9,11},{10,... | collective-permute-start | bytes 4718600 | tf_op jit(solution)/shard_map/ppermute | solution.py:458
  304.9 49.6 %collective-permute-start.39 = (f32[768,65]{1,0:T(8,128)}, f32[768,65]{1,0:T(8,128)}, u32[]{:S(2)}, u32[]{:S(2)}) collective-permute-start(f32[768,65]{1,0:T(8,128)} %pad_maximum_fusion.8), channel_id=1, source_target_pairs={{0,1},{1,0},{2,3},{3,2},{4,5},{5,4},{6,7},{7,6},{8,9},{9,8},{10,11... | collective-permute-start | bytes 599048 | tf_op jit(solution)/shard_map/ppermute | solution.py:458
  311.3 46.5 %collective-permute-start.37 = (bf16[512,768]{1,0:T(8,128)(2,1)}, bf16[512,768]{1,0:T(8,128)(2,1)}, u32[]{:S(2)}, u32[]{:S(2)}) collective-permute-start(bf16[512,768]{1,0:T(8,128)(2,1)} %fusion.92), channel_id=1, source_target_pairs={{0,2},{1,3},{2,0},{3,1},{4,6},{5,7},{6,4},{7,5},{8,10},{9,11},{10,... | collective-permute-start | bytes 2359304 | tf_op jit(solution)/shard_map/ppermute | solution.py:458
  312.6 64.6 %collective-permute-start.36 = (bf16[512,768]{1,0:T(8,128)(2,1)}, bf16[512,768]{1,0:T(8,128)(2,1)}, u32[]{:S(2)}, u32[]{:S(2)}) collective-permute-start(bf16[512,768]{1,0:T(8,128)(2,1)} %fusion.92), channel_id=1, source_target_pairs={{0,1},{1,0},{2,3},{3,2},{4,5},{5,4},{6,7},{7,6},{8,9},{9,8},{10,11... | collective-permute-start | bytes 2359304 | tf_op jit(solution)/shard_map/ppermute | solution.py:458
  316.2 50.9 %collective-permute-start.24 = (bf16[1,4,8,16,768]{4,3,2,1,0:T(8,128)(2,1)}, bf16[1,4,8,16,768]{4,3,2,1,0:T(8,128)(2,1)}, u32[]{:S(2)}, u32[]{:S(2)}) collective-permute-start(bf16[1,4,8,16,768]{4,3,2,1,0:T(8,128)(2,1)} %broadcast_select_fusion), channel_id=1, source_target_pairs={{0,16},{4,20},{8,24},{12,28},{16,0},{20,4},{24,8},{28,12},{1,17},{... | collective-permute-start | bytes 2359304 | tf_op jit(solution)/shard_map/ppermute | solution.py:458
  370.7 46.0 %collective-permute-start.25 = (bf16[2,2,8,16,768]{4,3,2,1,0:T(8,128)(2,1)}, bf16[2,2,8,16,768]{4,3,2,1,0:T(8,128)(2,1)}, u32[]{:S(2)}, u32[]{:S(2)}) collective-permute-start(bf16[2,2,8,16,768]{4,3,2,1,0:T(8,128)(2,1)} %broadcast_select_fusion.2), channel_id=1, source_target_pairs={{0,8},{4,12},{8,0},{12,4},{16,24},{20,28},{24,16},{28,20},{1,9},{5... | collective-permute-start | bytes 2359304 | tf_op jit(solution)/shard_map/ppermute | solution.py:458
  382.4 49.2 %all-to-all-start.4 = ((bf16[8,96,641]{2,1,0:T(8,128)(2,1)}), bf16[8,96,641]{2,1,0:T(8,128)(2,1)}, u32[]{:S(2)}, u32[]{:S(2)}) async-start(bf16[8,96,641]{2,1,0:T(8,128)(2,1)} %pad_maximum_fusion.4), calls=%async_computation.4 | async-start | bytes 2359296 | tf_op jit(solution)/shard_map/all_to_all | solution.py:477
  429.5 28.1 %collective-permute-start.42 = (bf16[512,768]{1,0:T(8,128)(2,1)}, bf16[512,768]{1,0:T(8,128)(2,1)}, u32[]{:S(2)}, u32[]{:S(2)}) collective-permute-start(bf16[512,768]{1,0:T(8,128)(2,1)} %get-tuple-element.171), channel_id=1, source_target_pairs={{0,1},{1,0},{2,3},{3,2},{4,5},{5,4},{6,7},{7,6},{8,9},{9,8},{10,11... | collective-permute-start | bytes 2359304 | tf_op jit(solution)/shard_map/ppermute | solution.py:458
  440.9 29.8 %collective-permute-start.26 = (bf16[4,1,8,16,768]{4,3,2,1,0:T(8,128)(2,1)}, bf16[4,1,8,16,768]{4,3,2,1,0:T(8,128)(2,1)}, u32[]{:S(2)}, u32[]{:S(2)}) collective-permute-start(bf16[4,1,8,16,768]{4,3,2,1,0:T(8,128)(2,1)} %bitcast_select_fusion.1), channel_id=1, source_target_pairs={{0,4},{4,0},{8,12},{12,8},{16,20},{20,16},{24,28},{28,24},{1,5},{5... | collective-permute-start | bytes 2359304 | tf_op jit(solution)/shard_map/ppermute | solution.py:458
  442.9 33.8 %collective-permute-start.41 = (bf16[512,768]{1,0:T(8,128)(2,1)}, bf16[512,768]{1,0:T(8,128)(2,1)}, u32[]{:S(2)}, u32[]{:S(2)}) collective-permute-start(bf16[512,768]{1,0:T(8,128)(2,1)} %get-tuple-element.170), channel_id=1, source_target_pairs={{0,1},{1,0},{2,3},{3,2},{4,5},{5,4},{6,7},{7,6},{8,9},{9,8},{10,11... | collective-permute-start | bytes 2359304 | tf_op jit(solution)/shard_map/ppermute | solution.py:458
  453.7 36.9 %all-to-all-start.6 = ((bf16[8,96,833]{2,1,0:T(8,128)(2,1)}), bf16[8,96,833]{2,1,0:T(8,128)(2,1)S(1)}, u32[]{:S(2)}, u32[]{:S(2)}) async-start(bf16[8,96,833]{2,1,0:T(8,128)(2,1)} %broadcast_in_dim.14), calls=%async_computation.6 | async-start | bytes 2752512 | tf_op jit(solution)/shard_map/all_to_all | solution.py:477
  (109 other events, 1138.3 us)

commit v2 on v1

--- a/solution.py
+++ b/solution.py
@@ -281,7 +281,7 @@
             ],
         ),
         compiler_params=params(),
-        cost_estimate=cost(1.4e10 * count, 5e6 * count),
+        cost_estimate=cost(2.2e10 * count, 5e6 * count),
         name="attend_back",
     )(*spans, qkv, grad_heads, head_out, norms, qkv, key_t, qkv, tiles, seg_col, seg_row, *ready)
 
@@ -369,7 +369,7 @@
         ],
         out_specs=slots + [kept(hidden_units), kept(hidden_units), kept(width), kept(expert_count)],
         compiler_params=params(),
-        cost_estimate=cost(6 * count * tiles * rows * width * hidden_units, 7e6 * count),
+        cost_estimate=cost(17 * count * tiles * rows * width * hidden_units, 7e6 * count),
         name="experts",
     )(*xs, *us, w_in, w_out, w_router, hots)
     return res[:groups], res[groups:]
@@ -443,7 +443,7 @@
         ],
         input_output_aliases={inputs + n: n for n in range(len(earlier))},
         compiler_params=params(),
-        cost_estimate=cost(6 * count * tiles * rows * width * hidden_units, 1e7 * count),
+        cost_estimate=cost(17 * count * tiles * rows * width * hidden_units, 1e7 * count),
         name="expert_weights",
     )(*xs, *kept, w_out, *earlier)
     return res[: groups + 2], res[groups + 2]

time: 506 us -> 529 us (1.045)
  Pallas kernels: 152 us -> 166 us
  local copies, waits for them, and re-layouts: 41.4 us -> 50.5 us
  waiting for transfers between devices: 144 us -> 152 us
  starting transfers between devices: 82.3 us -> 74.7 us
    ppermute x49, waiting for transfers between devices: 85.3 us -> 94.5 us  [swap(): return lax.ppermute(values, axis, [(n, n ^ step) for n in range(count)])]
    pallas_call x2, Pallas kernels: 48.3 us -> 57 us  [attend_back(): pl.pallas_call(lambda *refs: attend_back_kernel(count, head_dim, reach, f...]
    ppermute x49, starting transfers between devices: 41.3 us -> 33.7 us  [swap(): return lax.ppermute(values, axis, [(n, n ^ step) for n in range(count)])]
    unnamed x176 -> x166, local copies, waits for them, and re-layouts: 22.2 us -> 27.7 us
  transfers between devices with their start and end apart: 56 -> 56, of which waited for: 20 -> 17; matrix products, arithmetic and copies ran while one was open for 18% -> 18% of each run, Pallas kernels for 31% -> 32%
where the time goes in v2:
time: 529 us; the launch traced here: 522 us
  Pallas kernels  166 us (31%)
  waiting for transfers between devices  152 us (29%)
  starting transfers between devices  74.7 us (14%)
  local copies, waits for them, and re-layouts  50.5 us (10%)
  other arithmetic  42 us (8%)
  matrix products  33.1 us (6%)
    ppermute x49, waiting for transfers between devices, swap(): return lax.ppermute(values, axis, [(n, n ^ step) for n in range(count)])  94.5 us
    all_to_all x7, waiting for transfers between devices, trade_dp(): return lax.all_to_all(values, 'dp', split_axis=0, concat_axis=0, tiled=True)  57 us
    pallas_call x2, Pallas kernels, attend_back(): pl.pallas_call(lambda *refs: attend_back_kernel(count, head_dim, reach, f...  57 us
    all_to_all x7, starting transfers between devices, trade_dp(): return lax.all_to_all(values, 'dp', split_axis=0, concat_axis=0, tiled=True)  41 us
    pallas_call x2, Pallas kernels, experts(): pl.pallas_call(lambda *refs: expert_kernel(groups, *refs), out_shape=[jax...  36.9 us
    pallas_call x2, Pallas kernels, expert_weights(): pl.pallas_call(lambda *refs: weight_kernel(groups, *refs), out_shape=[jax...  34.4 us
    ppermute x49, starting transfers between devices, swap(): return lax.ppermute(values, axis, [(n, n ^ step) for n in range(count)])  33.7 us
    unnamed x166, local copies, waits for them, and re-layouts  27.7 us
  transfers between devices with their start and end apart: 56, of which 17 were waited for; matrix products, arithmetic and copies ran while one was open for 18% of the time, Pallas kernels for 32%

profile of v2, /device:TPU:0, one launch (start us, length us, event | category | flops | bytes accessed | tf_op | source)
XLA Modules:
  0.0 522.0 jit_solution(10627355807165118699)
XLA Ops:
  11.3 6.2 %all-to-all-start.1 = ((bf16[8,8,16,768]{3,2,1,0:T(8,128)(2,1)}), bf16[8,8,16,768]{3,2,1,0:T(8,128)(2,1)}, u32[]{:S(2)}, u32[]{:S(2)}) async-start(bf16[8,8,16,768]{3,2,1,0:T(8,128)(2,1)} %bitcast.10), calls=%async_computation.1 | async-start | bytes 3145728 | tf_op jit(solution)/shard_map/all_to_all | solution.py:477
  22.4 11.9 %bias_tiles.1.refs_6_.refs_10_ = f32[3,9,256,256]{3,2,1,0:T(8,128)} custom-call(f32[3,1,2560]{2,1,0:T(1,128)S(1)} %broadcast_in_dim.10.rows_ref), custom_call_target="tpu_custom_call" | custom-call | flops 100000000 | bytes 7077888 | tf_op jit(solution)/shard_map/bias_tiles/pallas_call | solution.py:68
  43.9 26.3 %attend.1 = (bf16[2048,256]{1,0:T(8,128)(2,1)S(1)}, f32[8,2048]{1,0:T(8,128)S(1)}) custom-call(s32[8]{0:T(128)S(1)} %get-tuple-element.217.refs_0_, s32[8]{0:T(128)S(1)} %get-tuple-element.216.refs_1_, s32[8]{0:T(128)S(1)} %fusion.82.refs_2_, bf16[2048,768]{1,0:T(8,128)(2,1)} %copy-done.48, bf16[2048,768]{1,0:T(8,128)(2,1)} %copy-done.48, ...), custom_call_target="tpu_custom_call" | custom-call | flops 20000000000 | bytes 12000000 | tf_op jit(solution)/shard_map/attend/pallas_call | solution.py:134
  72.7 6.5 %collective-permute-done.8 = bf16[512,192]{1,0:T(8,128)(2,1)S(1)} collective-permute-done((bf16[512,192]{1,0:T(8,128)(2,1)S(1)}, bf16[512,192]{1,0:T(8,128)(2,1)S(1)}, u32[]{:S(2)}, u32[]{:S(2)}) %collective-permute-start.8) | collective-permute-done | bytes 196640 | tf_op jit(solution)/shard_map/ppermute | solution.py:458
  79.3 5.8 %collective-permute-done.7 = bf16[512,192]{1,0:T(8,128)(2,1)S(1)} collective-permute-done((bf16[512,192]{1,0:T(8,128)(2,1)S(1)}, bf16[512,192]{1,0:T(8,128)(2,1)S(1)}, u32[]{:S(2)}, u32[]{:S(2)}) %collective-permute-start.7) | collective-permute-done | bytes 196640 | tf_op jit(solution)/shard_map/ppermute | solution.py:458
  90.9 7.7 %all-to-all-start = ((bf16[8,8,16,768]{3,2,1,0:T(8,128)(2,1)}), bf16[8,8,16,768]{3,2,1,0:T(8,128)(2,1)}, u32[]{:S(2)}, u32[]{:S(2)}) async-start(bf16[8,8,16,768]{3,2,1,0:T(8,128)(2,1)} %bitcast.9), calls=%async_computation | async-start | bytes 3145728 | tf_op jit(solution)/shard_map/all_to_all | solution.py:477
  99.2 36.5 %all-to-all-done = bf16[8,8,16,768]{3,2,1,0:T(8,128)(2,1)} async-done(((bf16[8,8,16,768]{3,2,1,0:T(8,128)(2,1)}), bf16[8,8,16,768]{3,2,1,0:T(8,128)(2,1)}, u32[]{:S(2)}, u32[]{:S(2)}) %all-to-all-start) | async-done | bytes 1572896 | tf_op jit(solution)/shard_map/all_to_all | solution.py:477
  141.1 16.8 %collective-permute-done.13.refs_2_ = bf16[8,4,16,768]{3,2,1,0:T(8,128)(2,1)} collective-permute-done((bf16[8,4,16,768]{3,2,1,0:T(8,128)(2,1)S(1)}, bf16[8,4,16,768]{3,2,1,0:T(8,128)(2,1)}, u32[]{:S(2)}, u32[]{:S(2)}) %collective-permute-start.13) | collective-permute-done | bytes 786464 | tf_op jit(solution)/shard_map/ppermute | solution.py:458
  159.6 12.8 %collective-permute-done.19.refs_2_ = bf16[8,4,16,768]{3,2,1,0:T(8,128)(2,1)S(1)} collective-permute-done((bf16[8,4,16,768]{3,2,1,0:T(8,128)(2,1)S(1)}, bf16[8,4,16,768]{3,2,1,0:T(8,128)(2,1)S(1)}, u32[]{:S(2)}, u32[]{:S(2)}) %collective-permute-start.19) | collective-permute-done | bytes 786464 | tf_op jit(solution)/shard_map/ppermute | solution.py:458
  173.7 18.5 %experts.2 = (bf16[8,4,16,768]{3,2,1,0:T(8,128)(2,1)S(1)}, bf16[8,4,16,768]{3,2,1,0:T(8,128)(2,1)S(1)}, bf16[8,4,16,768]{3,2,1,0:T(8,128)(2,1)S(1)}, bf16[8,4,16...) custom-call(bf16[8,4,16,768]{3,2,1,0:T(8,128)(2,1)} %copy-done.3, ...), custom_call_target="tpu_custom_call" | custom-call | flops 20535312384 | bytes 28000000 | tf_op jit(solution)/shard_map/experts/pallas_call | solution.py:352
  194.6 18.4 %experts.3 = (bf16[8,4,16,768]{3,2,1,0:T(8,128)(2,1)S(1)}, bf16[8,4,16,768]{3,2,1,0:T(8,128)(2,1)}, bf16[8,4,16,768]{3,2,1,0:T(8,128)(2,1)S(1)}, bf16[8,4,16,768...) custom-call(bf16[8,4,16,768]{3,2,1,0:T(8,128)(2,1)} %copy-done.5, ...), custom_call_target="tpu_custom_call" | custom-call | flops 20535312384 | bytes 28000000 | tf_op jit(solution)/shard_map/experts/pallas_call | solution.py:352
  215.7 17.0 %expert_weights.2 = (bf16[8,8,16,768]{3,2,1,0:T(8,128)(2,1)}, bf16[8,8,16,768]{3,2,1,0:T(8,128)(2,1)}, bf16[8,8,16,768]{3,2,1,0:T(8,128)(2,1)}, bf16[8,8,16,768]...) custom-call(bf16[8,4,16,768]{3,2,1,0:T(8,128)(2,1)S(1)} %copy-done.6, ...), custom_call_target="tpu_custom_call" | custom-call | flops 20535312384 | bytes 40000000 | tf_op jit(solution)/shard_map/expert_weights/pallas_call | solution.py:425
  236.3 5.3 %all-to-all-start.3 = ((bf16[8,4,16,768]{3,2,1,0:T(8,128)(2,1)}), bf16[8,4,16,768]{3,2,1,0:T(8,128)(2,1)}, u32[]{:S(2)}, u32[]{:S(2)}) async-start(bf16[8,4,16,768]{3,2,1,0:T(8,128)(2,1)} %add_convert_fusion.3), calls=%async_computation.3 | async-start | bytes 1572864 | tf_op jit(solution)/shard_map/all_to_all | solution.py:477
  243.9 17.4 %expert_weights.3 = (bf16[8,8,16,768]{3,2,1,0:T(8,128)(2,1)}, bf16[8,8,16,768]{3,2,1,0:T(8,128)(2,1)}, bf16[8,8,16,768]{3,2,1,0:T(8,128)(2,1)}, bf16[8,8,16,768]...) custom-call(bf16[8,4,16,768]{3,2,1,0:T(8,128)(2,1)S(1)} %copy-done.4, ...), custom_call_target="tpu_custom_call", output_to_operand_aliasing={{0}: (9, {}), {1}: (10, {}), {2}: (11, {}), {3}: (12, {}), ... | custom-call | flops 20535312384 | bytes 40000000 | tf_op jit(solution)/shard_map/expert_weights/pallas_call | solution.py:425
  265.4 6.1 %all-to-all-start.2 = ((bf16[8,4,16,768]{3,2,1,0:T(8,128)(2,1)}), bf16[8,4,16,768]{3,2,1,0:T(8,128)(2,1)}, u32[]{:S(2)}, u32[]{:S(2)}) async-start(bf16[8,4,16,768]{3,2,1,0:T(8,128)(2,1)} %add_convert_fusion.5), calls=%async_computation.2 | async-start | bytes 1572864 | tf_op jit(solution)/shard_map/all_to_all | solution.py:477
  284.0 8.4 %all-to-all-done.2 = bf16[8,4,16,768]{3,2,1,0:T(8,128)(2,1)} async-done(((bf16[8,4,16,768]{3,2,1,0:T(8,128)(2,1)}), bf16[8,4,16,768]{3,2,1,0:T(8,128)(2,1)}, u32[]{:S(2)}, u32[]{:S(2)}) %all-to-all-start.2) | async-done | bytes 786464 | tf_op jit(solution)/shard_map/all_to_all | solution.py:477
  307.4 17.7 %collective-permute-done.35 = bf16[512,192]{1,0:T(8,128)(2,1)S(1)} collective-permute-done((bf16[512,192]{1,0:T(8,128)(2,1)S(1)}, bf16[512,192]{1,0:T(8,128)(2,1)S(1)}, u32[]{:S(2)}, u32[]{:S(2)}) %collective-permute-start.35) | collective-permute-done | bytes 196640 | tf_op jit(solution)/shard_map/ppermute | solution.py:458
  338.9 34.7 %attend_back.2 = (bf16[2048,128]{1,0:T(8,128)(2,1)S(1)}, bf16[2048,128]{1,0:T(8,128)(2,1)S(1)}, bf16[2048,128]{1,0:T(8,128)(2,1)S(1)}, f32[8,2560]{1,0:T(8,128)S(1)}) custom-call(s32[8]{0:T(128)S(1)} %get-tuple-element.217.refs_0_, s32[8]{0:T(128)S(1)} %get-tuple-element.216.refs_1_, s32[8]{0:T(128)S(1)} %fusion.82.refs_2_, bf16[2048,768]{1,0:T(8,128)(2,1)} %copy-done.48, ...), custom_call_target="tpu_custom_call" | custom-call | flops 44000002048 | bytes 10000000 | tf_op jit(solution)/shard_map/attend_back/pallas_call | solution.py:247
  383.4 9.1 %collective-permute-done.40 = f32[768,65]{1,0:T(8,128)S(1)} collective-permute-done((f32[768,65]{1,0:T(8,128)S(1)}, f32[768,65]{1,0:T(8,128)S(1)}, u32[]{:S(2)}, u32[]{:S(2)}) %collective-permute-start.40) | collective-permute-done | bytes 199712 | tf_op jit(solution)/shard_map/ppermute | solution.py:458
  401.4 5.4 %all-to-all-start.4 = ((bf16[8,96,641]{2,1,0:T(8,128)(2,1)}), bf16[8,96,641]{2,1,0:T(8,128)(2,1)}, u32[]{:S(2)}, u32[]{:S(2)}) async-start(bf16[8,96,641]{2,1,0:T(8,128)(2,1)} %pad_maximum_fusion.4), calls=%async_computation.4 | async-start | bytes 2359296 | tf_op jit(solution)/shard_map/all_to_all | solution.py:477
  406.9 22.2 %attend_back.3 = (bf16[2048,128]{1,0:T(8,128)(2,1)S(1)}, bf16[2048,128]{1,0:T(8,128)(2,1)S(1)}, bf16[2048,128]{1,0:T(8,128)(2,1)S(1)}, f32[8,2560]{1,0:T(8,128)S(1)}) custom-call(s32[8]{0:T(128)S(1)} %get-tuple-element.217.refs_0_, s32[8]{0:T(128)S(1)} %get-tuple-element.216.refs_1_, s32[8]{0:T(128)S(1)} %fusion.82.refs_2_, bf16[2048,768]{1,0:T(8,128)(2,1)} %copy-done.48, ...), custom_call_target="tpu_custom_call" | custom-call | flops 22000001024 | bytes 5000000 | tf_op jit(solution)/shard_map/attend_back/pallas_call | solution.py:247
  455.3 5.7 %all-to-all-start.5 = ((bf16[8,96,192]{1,2,0:T(8,128)(2,1)}), bf16[8,96,192]{1,2,0:T(8,128)(2,1)S(1)}, u32[]{:S(2)}, u32[]{:S(2)}) async-start(bf16[8,96,192]{1,2,0:T(8,128)(2,1)} %maximum_select_fusion), calls=%async_computation.5 | async-start | bytes 786432 | tf_op jit(solution)/shard_map/all_to_all | solution.py:477
  482.3 9.9 %collective-permute-done.26 = bf16[4,1,8,16,768]{4,3,2,1,0:T(8,128)(2,1)S(1)} collective-permute-done((bf16[4,1,8,16,768]{4,3,2,1,0:T(8,128)(2,1)}, bf16[4,1,8,16,768]{4,3,2,1,0:T(8,128)(2,1)S(1)}, u32[]{:S(2)}, u32[]{:S(2)}) %collective-permute-start.26) | collective-permute-done | bytes 786464 | tf_op jit(solution)/shard_map/ppermute | solution.py:458
  504.6 7.0 %all-to-all-done.6 = bf16[8,96,833]{2,1,0:T(8,128)(2,1)} async-done(((bf16[8,96,833]{2,1,0:T(8,128)(2,1)}), bf16[8,96,833]{2,1,0:T(8,128)(2,1)}, u32[]{:S(2)}, u32[]{:S(2)}) %all-to-all-start.6) | async-done | bytes 1279520 | tf_op jit(solution)/shard_map/all_to_all | solution.py:477
  (389 shorter events, 184.7 us)
Async XLA Ops:
  11.3 79.5 %all-to-all-start.1 = ((bf16[8,8,16,768]{3,2,1,0:T(8,128)(2,1)}), bf16[8,8,16,768]{3,2,1,0:T(8,128)(2,1)}, u32[]{:S(2)}, u32[]{:S(2)}) async-start(bf16[8,8,16,768]{3,2,1,0:T(8,128)(2,1)} %bitcast.10), calls=%async_computation.1 | async-start | bytes 3145728 | tf_op jit(solution)/shard_map/all_to_all | solution.py:477
  36.8 33.4 %collective-permute-start.10 = (bf16[192,768]{1,0:T(8,128)(2,1)}, bf16[192,768]{1,0:T(8,128)(2,1)}, u32[]{:S(2)}, u32[]{:S(2)}) collective-permute-start(bf16[192,768]{1,0:T(8,128)(2,1)} %param.21), channel_id=1, source_target_pairs={{0,2},{1,3},{2,0},{3,1},{4,6},{5,7},{6,4},{7,5},{8,10},{9,11},{10,... | collective-permute-start | bytes 884744 | tf_op jit(solution)/shard_map/ppermute | solution.py:458
  38.3 46.8 %collective-permute-start.9 = (bf16[192,768]{1,0:T(8,128)(2,1)}, bf16[192,768]{1,0:T(8,128)(2,1)}, u32[]{:S(2)}, u32[]{:S(2)}) collective-permute-start(bf16[192,768]{1,0:T(8,128)(2,1)} %param.21), channel_id=1, source_target_pairs={{0,1},{1,0},{2,3},{3,2},{4,5},{5,4},{6,7},{7,6},{8,9},{9,8},{10,11... | collective-permute-start | bytes 884744 | tf_op jit(solution)/shard_map/ppermute | solution.py:458
  90.9 44.9 %all-to-all-start = ((bf16[8,8,16,768]{3,2,1,0:T(8,128)(2,1)}), bf16[8,8,16,768]{3,2,1,0:T(8,128)(2,1)}, u32[]{:S(2)}, u32[]{:S(2)}) async-start(bf16[8,8,16,768]{3,2,1,0:T(8,128)(2,1)} %bitcast.9), calls=%async_computation | async-start | bytes 3145728 | tf_op jit(solution)/shard_map/all_to_all | solution.py:477
  98.6 39.2 %collective-permute-start.16 = (bf16[8,8,16,768]{3,2,1,0:T(8,128)(2,1)}, bf16[8,8,16,768]{3,2,1,0:T(8,128)(2,1)}, u32[]{:S(2)}, u32[]{:S(2)}) collective-permute-start(bf16[8,8,16,768]{3,2,1,0:T(8,128)(2,1)} %all-to-all-done.1.refs_4_), channel_id=1, source_target_pairs={{0,2},{1,3},{2,0},{3,1},{4,6},{5,7},{6,4},{7,5},{8,10},{9,11},{10,... | collective-permute-start | bytes 4718600 | tf_op jit(solution)/shard_map/ppermute | solution.py:458
  137.9 34.6 %collective-permute-start.17 = (bf16[8,8,16,768]{3,2,1,0:T(8,128)(2,1)}, bf16[8,8,16,768]{3,2,1,0:T(8,128)(2,1)}, u32[]{:S(2)}, u32[]{:S(2)}) collective-permute-start(bf16[8,8,16,768]{3,2,1,0:T(8,128)(2,1)} %collective-permute-done.16.refs_6_), channel_id=1, source_target_pairs={{0,1},{1,0},{2,3},{3,2},{4,5},{5,4},{6,7},{7,6},{8,9},{9,8},{10,11... | collective-permute-start | bytes 4718600 | tf_op jit(solution)/shard_map/ppermute | solution.py:458
  139.4 33.0 %collective-permute-start.12 = (bf16[8,4,16,768]{3,2,1,0:T(8,128)(2,1)S(1)}, bf16[8,4,16,768]{3,2,1,0:T(8,128)(2,1)S(1)}, u32[]{:S(2)}, u32[]{:S(2)}) collective-permute-start(bf16[8,4,16,768]{3,2,1,0:T(8,128)(2,1)S(1)} %get-tuple-element.186.refs_0_), channel_id=1, source_target_pairs={{0,1},{1,0},{2,3},{3,2},{4,5},{5,4},{6,7},{7,6},{8,9},{9,8},{10,11... | collective-permute-start | bytes 2359304 | tf_op jit(solution)/shard_map/ppermute | solution.py:458
  139.5 32.9 %collective-permute-start.19 = (bf16[8,4,16,768]{3,2,1,0:T(8,128)(2,1)S(1)}, bf16[8,4,16,768]{3,2,1,0:T(8,128)(2,1)S(1)}, u32[]{:S(2)}, u32[]{:S(2)}) collective-permute-start(bf16[8,4,16,768]{3,2,1,0:T(8,128)(2,1)S(1)} %get-tuple-element.185.refs_0_), channel_id=1, source_target_pairs={{0,2},{1,3},{2,0},{3,1},{4,6},{5,7},{6,4},{7,5},{8,10},{9,11},{10,... | collective-permute-start | bytes 2359304 | tf_op jit(solution)/shard_map/ppermute | solution.py:458
  159.0 33.8 %collective-permute-start.18 = (bf16[8,4,16,768]{3,2,1,0:T(8,128)(2,1)S(1)}, bf16[8,4,16,768]{3,2,1,0:T(8,128)(2,1)S(1)}, u32[]{:S(2)}, u32[]{:S(2)}) collective-permute-start(bf16[8,4,16,768]{3,2,1,0:T(8,128)(2,1)S(1)} %get-tuple-element.185.refs_0_), channel_id=1, source_target_pairs={{0,1},{1,0},{2,3},{3,2},{4,5},{5,4},{6,7},{7,6},{8,9},{9,8},{10,11... | collective-permute-start | bytes 2359304 | tf_op jit(solution)/shard_map/ppermute | solution.py:458
  192.2 42.9 %collective-permute-start.30 = (bf16[8,4,16,768]{3,2,1,0:T(8,128)(2,1)S(1)}, bf16[8,4,16,768]{3,2,1,0:T(8,128)(2,1)S(1)}, u32[]{:S(2)}, u32[]{:S(2)}) collective-permute-start(bf16[8,4,16,768]{3,2,1,0:T(8,128)(2,1)S(1)} %get-tuple-element.85), channel_id=1, source_target_pairs={{0,1},{1,0},{2,3},{3,2},{4,5},{5,4},{6,7},{7,6},{8,9},{9,8},{10,11... | collective-permute-start | bytes 2359304 | tf_op jit(solution)/shard_map/ppermute | solution.py:458
  213.0 49.7 %collective-permute-start.27 = (bf16[8,4,16,768]{3,2,1,0:T(8,128)(2,1)}, bf16[8,4,16,768]{3,2,1,0:T(8,128)(2,1)}, u32[]{:S(2)}, u32[]{:S(2)}) collective-permute-start(bf16[8,4,16,768]{3,2,1,0:T(8,128)(2,1)} %get-tuple-element.81), channel_id=1, source_target_pairs={{0,1},{1,0},{2,3},{3,2},{4,5},{5,4},{6,7},{7,6},{8,9},{9,8},{10,11... | collective-permute-start | bytes 2359304 | tf_op jit(solution)/shard_map/ppermute | solution.py:458
  236.3 29.1 %all-to-all-start.3 = ((bf16[8,4,16,768]{3,2,1,0:T(8,128)(2,1)}), bf16[8,4,16,768]{3,2,1,0:T(8,128)(2,1)}, u32[]{:S(2)}, u32[]{:S(2)}) async-start(bf16[8,4,16,768]{3,2,1,0:T(8,128)(2,1)} %add_convert_fusion.3), calls=%async_computation.3 | async-start | bytes 1572864 | tf_op jit(solution)/shard_map/all_to_all | solution.py:477
  279.1 53.3 %collective-permute-start.21 = (bf16[8,8,16,768]{3,2,1,0:T(8,128)(2,1)}, bf16[8,8,16,768]{3,2,1,0:T(8,128)(2,1)}, u32[]{:S(2)}, u32[]{:S(2)}) collective-permute-start(bf16[8,8,16,768]{3,2,1,0:T(8,128)(2,1)} %get-tuple-element.77), channel_id=1, source_target_pairs={{0,1},{1,0},{2,3},{3,2},{4,5},{5,4},{6,7},{7,6},{8,9},{9,8},{10,11... | collective-permute-start | bytes 4718600 | tf_op jit(solution)/shard_map/ppermute | solution.py:458
  283.3 49.1 %collective-permute-start.23 = (bf16[8,8,16,768]{3,2,1,0:T(8,128)(2,1)}, bf16[8,8,16,768]{3,2,1,0:T(8,128)(2,1)}, u32[]{:S(2)}, u32[]{:S(2)}) collective-permute-start(bf16[8,8,16,768]{3,2,1,0:T(8,128)(2,1)} %add_convert_fusion.1.refs_13_), channel_id=1, source_target_pairs={{0,2},{1,3},{2,0},{3,1},{4,6},{5,7},{6,4},{7,5},{8,10},{9,11},{10,... | collective-permute-start | bytes 4718600 | tf_op jit(solution)/shard_map/ppermute | solution.py:458
  325.1 54.8 %collective-permute-start.39 = (f32[768,65]{1,0:T(8,128)}, f32[768,65]{1,0:T(8,128)}, u32[]{:S(2)}, u32[]{:S(2)}) collective-permute-start(f32[768,65]{1,0:T(8,128)} %pad_maximum_fusion.8), channel_id=1, source_target_pairs={{0,1},{1,0},{2,3},{3,2},{4,5},{5,4},{6,7},{7,6},{8,9},{9,8},{10,11... | collective-permute-start | bytes 599048 | tf_op jit(solution)/shard_map/ppermute | solution.py:458
  331.6 51.8 %collective-permute-start.37 = (bf16[512,768]{1,0:T(8,128)(2,1)}, bf16[512,768]{1,0:T(8,128)(2,1)}, u32[]{:S(2)}, u32[]{:S(2)}) collective-permute-start(bf16[512,768]{1,0:T(8,128)(2,1)} %fusion.92), channel_id=1, source_target_pairs={{0,2},{1,3},{2,0},{3,1},{4,6},{5,7},{6,4},{7,5},{8,10},{9,11},{10,... | collective-permute-start | bytes 2359304 | tf_op jit(solution)/shard_map/ppermute | solution.py:458
  332.4 63.7 %collective-permute-start.36 = (bf16[512,768]{1,0:T(8,128)(2,1)}, bf16[512,768]{1,0:T(8,128)(2,1)}, u32[]{:S(2)}, u32[]{:S(2)}) collective-permute-start(bf16[512,768]{1,0:T(8,128)(2,1)} %fusion.92), channel_id=1, source_target_pairs={{0,1},{1,0},{2,3},{3,2},{4,5},{5,4},{6,7},{7,6},{8,9},{9,8},{10,11... | collective-permute-start | bytes 2359304 | tf_op jit(solution)/shard_map/ppermute | solution.py:458
  336.0 56.6 %collective-permute-start.24 = (bf16[1,4,8,16,768]{4,3,2,1,0:T(8,128)(2,1)}, bf16[1,4,8,16,768]{4,3,2,1,0:T(8,128)(2,1)}, u32[]{:S(2)}, u32[]{:S(2)}) collective-permute-start(bf16[1,4,8,16,768]{4,3,2,1,0:T(8,128)(2,1)} %broadcast_select_fusion), channel_id=1, source_target_pairs={{0,16},{4,20},{8,24},{12,28},{16,0},{20,4},{24,8},{28,12},{1,17},{... | collective-permute-start | bytes 2359304 | tf_op jit(solution)/shard_map/ppermute | solution.py:458
  396.1 40.3 %collective-permute-start.25 = (bf16[2,2,8,16,768]{4,3,2,1,0:T(8,128)(2,1)}, bf16[2,2,8,16,768]{4,3,2,1,0:T(8,128)(2,1)}, u32[]{:S(2)}, u32[]{:S(2)}) collective-permute-start(bf16[2,2,8,16,768]{4,3,2,1,0:T(8,128)(2,1)} %broadcast_select_fusion.2), channel_id=1, source_target_pairs={{0,8},{4,12},{8,0},{12,4},{16,24},{20,28},{24,16},{28,20},{1,9},{5... | collective-permute-start | bytes 2359304 | tf_op jit(solution)/shard_map/ppermute | solution.py:458
  401.4 49.8 %all-to-all-start.4 = ((bf16[8,96,641]{2,1,0:T(8,128)(2,1)}), bf16[8,96,641]{2,1,0:T(8,128)(2,1)}, u32[]{:S(2)}, u32[]{:S(2)}) async-start(bf16[8,96,641]{2,1,0:T(8,128)(2,1)} %pad_maximum_fusion.4), calls=%async_computation.4 | async-start | bytes 2359296 | tf_op jit(solution)/shard_map/all_to_all | solution.py:477
  450.1 29.2 %collective-permute-start.42 = (bf16[512,768]{1,0:T(8,128)(2,1)}, bf16[512,768]{1,0:T(8,128)(2,1)}, u32[]{:S(2)}, u32[]{:S(2)}) collective-permute-start(bf16[512,768]{1,0:T(8,128)(2,1)} %get-tuple-element.171), channel_id=1, source_target_pairs={{0,1},{1,0},{2,3},{3,2},{4,5},{5,4},{6,7},{7,6},{8,9},{9,8},{10,11... | collective-permute-start | bytes 2359304 | tf_op jit(solution)/shard_map/ppermute | solution.py:458
  462.0 30.2 %collective-permute-start.26 = (bf16[4,1,8,16,768]{4,3,2,1,0:T(8,128)(2,1)}, bf16[4,1,8,16,768]{4,3,2,1,0:T(8,128)(2,1)S(1)}, u32[]{:S(2)}, u32[]{:S(2)}) collective-permute-start(bf16[4,1,8,16,768]{4,3,2,1,0:T(8,128)(2,1)} %bitcast_select_fusion.1), channel_id=1, source_target_pairs={{0,4},{4,0},{8,12},{12,8},{16,20},{20,16},{24,28},{28,24},{1,5},{5... | collective-permute-start | bytes 2359304 | tf_op jit(solution)/shard_map/ppermute | solution.py:458
  464.0 31.9 %collective-permute-start.41 = (bf16[512,768]{1,0:T(8,128)(2,1)}, bf16[512,768]{1,0:T(8,128)(2,1)}, u32[]{:S(2)}, u32[]{:S(2)}) collective-permute-start(bf16[512,768]{1,0:T(8,128)(2,1)} %get-tuple-element.170), channel_id=1, source_target_pairs={{0,1},{1,0},{2,3},{3,2},{4,5},{5,4},{6,7},{7,6},{8,9},{9,8},{10,11... | collective-permute-start | bytes 2359304 | tf_op jit(solution)/shard_map/ppermute | solution.py:458
  474.8 36.8 %all-to-all-start.6 = ((bf16[8,96,833]{2,1,0:T(8,128)(2,1)}), bf16[8,96,833]{2,1,0:T(8,128)(2,1)}, u32[]{:S(2)}, u32[]{:S(2)}) async-start(bf16[8,96,833]{2,1,0:T(8,128)(2,1)} %broadcast_in_dim.14), calls=%async_computation.6 | async-start | bytes 2752512 | tf_op jit(solution)/shard_map/all_to_all | solution.py:477
  (104 other events, 1205.8 us)
